TPU v7x, 32 devices: a whole 2x2x4 slice. The times are simulated.
32 devices in a mesh: grp: 2 (over y), tm: 8 (over z, x), unit: 2 (over core).
Axes of the slice: x: 2, y: 2, z: 4, core: 2. Of those that a mesh axis runs over, the one named last changes fastest.
Arguments:
- panel_data: bfloat16 [1024, 64], P(('grp', 'tm', 'unit')), parts along dimension 0, may hold values from -6 to 6
- cell_mask: int32 [8, 64], P('grp'), parts along dimension 0, may hold values 0 or 1
- loadings: bfloat16 [512, 128], replicated, may hold values from -1 to 1
- noise_prec: float32 [512], replicated, may hold values from 0.5 to 4
- transition: float32 [128, 128], replicated, may hold values from -1 to 1, as said below
- proc_var: float32 [128], replicated, may hold values from 0.00625 to 2
- prior_mean: float32 [128], replicated, may hold values from -6 to 6
Outputs:
- smoothed_mean: float32 [128, 128], P(('grp', 'tm')), parts along dimension 0
- smoothed_var: float32 [128, 128], P(('grp', 'tm')), parts along dimension 0
There are 2 independent parts, one for each index of `grp`. A program takes and returns all parts, laid end to end along the dimension named above; an argument that names none is the same for every part. Nothing has to cross between parts.
Inputs may be any that keep to these rules, and one draw needn't show every extreme that they name: transition is lower triangular with diagonal entries in (0, 1).
All inputs are finite; a program needn't handle non-finite values.
Results may differ from a plain program's by a relative error of at most 0.003.
Values may be sent and summed in bfloat16 or wider, within the bound.
No kernel may reach another device: no remote copies, remote signals or barrier semaphores. Data moves between devices by JAX's collectives and lax.ppermute only.
A program may use at most 128 MiB of HBM per device.

v0:
```python
import jax
import jax.numpy as jnp
from jax import lax
from jax.sharding import PartitionSpec as P

BLOCK = 128


HIGHEST = lax.Precision.HIGHEST


def carried_in(value, axis, join, neutral, backward):
    count, mine = (lax.axis_size(axis), lax.axis_index(axis))
    pieces = jax.tree.map(lambda part: lax.all_gather(part, axis), value)
    if backward:
        pieces = jax.tree.map(lambda part: part[::-1], pieces)
        mine = count - 1 - mine
    running = jax.tree.map(
        lambda part, zero: jnp.full_like(part, 0) + jnp.asarray(zero, part.dtype), value, neutral
    )

    def step(position, running):
        longer = join(running, jax.tree.map(lambda part: part[position], pieces))
        return jax.tree.map(lambda new, old: jnp.where(position < mine, new, old), longer, running)

    return lax.fori_loop(0, count - 1, step, running)


def product(left, right):
    return jnp.matmul(left, right, precision=HIGHEST)


def mat_vec(matrix, vector):
    return jnp.einsum("...kl,...l->...k", matrix, vector, precision=HIGHEST)


def flipped(matrix):
    return jnp.swapaxes(matrix, -1, -2)


def chol_apply(factor, rhs):
    middle = lax.linalg.triangular_solve(factor, rhs, left_side=True, lower=True)
    return lax.linalg.triangular_solve(factor, middle, left_side=True, lower=True, transpose_a=True)


def filter_join(earlier, later):
    trans_one, shift_one, cov_one, info_one, vec_one, live_one = earlier
    trans_two, shift_two, cov_two, info_two, vec_two, live_two = later
    identity_mat = jnp.eye(trans_one.shape[-1], dtype=jnp.float32)
    live_mat = live_one[..., None, None]
    factor_one = jnp.linalg.cholesky(cov_one + (1.0 - live_mat) * identity_mat)
    inner_mat = identity_mat + product(product(flipped(factor_one), info_two), factor_one)
    inner_factor = jnp.linalg.cholesky(inner_mat)
    solved = lax.linalg.triangular_solve(
        inner_factor, flipped(factor_one), left_side=True, lower=True
    )
    spread_mat = product(trans_two, flipped(solved))
    pushed = product(info_two, trans_one)
    reduced = product(solved, pushed)
    residue = vec_two - mat_vec(info_two, shift_one)
    solved_residue = mat_vec(solved, residue)
    trans_new = product(trans_two, trans_one) - product(spread_mat, reduced)
    shift_new = mat_vec(trans_two, shift_one) + mat_vec(spread_mat, solved_residue) + shift_two
    cov_new = product(spread_mat, flipped(spread_mat)) + cov_two
    info_new = product(flipped(trans_one), pushed) - product(flipped(reduced), reduced) + info_one
    vec_new = (
        mat_vec(flipped(trans_one), residue) - mat_vec(flipped(reduced), solved_residue) + vec_one
    )
    alive_mat = live_mat > 0.5
    alive_vec = live_one[..., None] > 0.5
    return (
        jnp.where(alive_mat, trans_new, trans_two),
        jnp.where(alive_vec, shift_new, shift_two),
        jnp.where(alive_mat, cov_new, cov_two),
        jnp.where(alive_mat, info_new, info_two),
        jnp.where(alive_vec, vec_new, vec_two),
        jnp.maximum(live_one, live_two),
    )


def smooth_join(lower_elem, higher_elem):
    gain_low, offset_low, cov_low = lower_elem
    gain_high, offset_high, cov_high = higher_elem
    return (
        product(gain_low, gain_high),
        mat_vec(gain_low, offset_high) + offset_low,
        product(product(gain_low, cov_high), flipped(gain_low)) + cov_low,
    )


def smooth_scan_join(earlier, later):
    return smooth_join(later, earlier)


def take_last(stacked):
    return stacked[-1]


def take_first(stacked):
    return stacked[0]


def per_device(panel_data, cell_mask, loadings, noise_prec, transition, proc_var, prior_mean):
    n_time = lax.axis_size("tm")
    n_unit = lax.axis_size("unit")
    time_index = lax.axis_index("tm")
    unit_index = lax.axis_index("unit")
    rows_own, total_time = panel_data.shape
    steps = total_time // n_time
    width = transition.shape[0]
    identity_mat = jnp.eye(width, dtype=jnp.float32)
    my_columns = lax.dynamic_slice_in_dim(cell_mask, time_index * steps, steps, 1)
    half_load = lax.dynamic_index_in_dim(
        loadings.reshape(n_time, n_unit, rows_own, width), unit_index, 1, keepdims=False
    ).reshape(n_time * rows_own, width)
    half_prec = lax.dynamic_index_in_dim(
        noise_prec.reshape(n_time, n_unit, rows_own), unit_index, 1, keepdims=False
    ).reshape(n_time * rows_own)
    half_ids = (
        (jnp.arange(n_time, dtype=jnp.int32)[:, None] * n_unit + unit_index) * rows_own
        + jnp.arange(rows_own, dtype=jnp.int32)[None, :]
    ).reshape(-1)
    half_weighted = (half_prec[:, None] * half_load.astype(jnp.float32)).astype(jnp.bfloat16)
    half_mask = jnp.take(my_columns, half_ids // BLOCK, axis=0).astype(jnp.bfloat16)
    regrouped = lax.all_to_all(panel_data, "tm", split_axis=1, concat_axis=0, tiled=True)
    vec_half = jnp.dot((half_mask * regrouped).T, half_weighted, preferred_element_type=jnp.float32)
    group_rows = min(rows_own, BLOCK)
    n_groups = n_time * rows_own // group_rows
    group_gram = jnp.einsum(
        "gnk,gnl->gkl",
        half_weighted.reshape(n_groups, group_rows, width),
        half_load.reshape(n_groups, group_rows, width),
        preferred_element_type=jnp.float32,
    )
    group_block = half_ids.reshape(n_groups, group_rows)[:, 0] // BLOCK
    group_mask = jnp.take(my_columns, group_block, axis=0).astype(jnp.float32)
    info_half = jnp.einsum("gt,gkl->tkl", group_mask, group_gram, precision=HIGHEST)
    info_mat, info_vec = lax.psum((info_half, vec_half), "unit")
    global_step = time_index * steps + jnp.arange(steps, dtype=jnp.int32)
    first_step = (global_step == 0).astype(jnp.float32)
    keep_step = 1.0 - first_step
    last_keep = 1.0 - (global_step == total_time - 1).astype(jnp.float32)
    inv_var = 1.0 / proc_var
    prior_prec = first_step[:, None, None] * identity_mat + keep_step[:, None, None] * jnp.diag(
        inv_var
    )
    eyes = jnp.broadcast_to(identity_mat, info_mat.shape)
    post_cov = chol_apply(jnp.linalg.cholesky(prior_prec + info_mat), eyes)
    shift_vec = jnp.einsum(
        "skl,sl->sk",
        post_cov,
        info_vec + first_step[:, None] * prior_mean[None, :],
        precision=HIGHEST,
    )
    scaled_trans = inv_var[:, None] * transition
    trans_part = keep_step[:, None, None] * jnp.einsum(
        "skl,lm->skm", post_cov, scaled_trans, precision=HIGHEST
    )
    middle = jnp.diag(inv_var)[None] - inv_var[None, :, None] * post_cov * inv_var[None, None, :]
    pressed = jnp.einsum("slm,mn->sln", middle, transition, precision=HIGHEST)
    info_part = keep_step[:, None, None] * jnp.einsum(
        "lk,sln->skn", transition, pressed, precision=HIGHEST
    )
    vec_part = keep_step[:, None] * jnp.einsum(
        "lk,sl->sk", transition, inv_var[None, :] * shift_vec, precision=HIGHEST
    )
    elements = (
        trans_part,
        shift_vec,
        post_cov,
        info_part,
        vec_part,
        jnp.ones((steps,), jnp.float32),
    )
    zero_vec = jnp.zeros((width,), jnp.float32)
    zero_mat = jnp.zeros((width, width), jnp.float32)
    filter_identity = (identity_mat, zero_vec, zero_mat, zero_mat, zero_vec, jnp.float32(0.0))
    local_joined = lax.associative_scan(filter_join, elements)
    filter_total = jax.tree.map(take_last, local_joined)
    before = carried_in(filter_total, "tm", filter_join, filter_identity, False)
    filtered = jax.vmap(filter_join, in_axes=(None, 0))(before, local_joined)
    filt_mean = filtered[1]
    filt_cov = filtered[2]
    moved_cov = jnp.einsum("kl,slm->skm", transition, filt_cov, precision=HIGHEST)
    pred_next = (
        jnp.einsum("skm,nm->skn", moved_cov, transition, precision=HIGHEST)
        + jnp.diag(proc_var)[None]
    )
    gain = (
        jnp.transpose(chol_apply(jnp.linalg.cholesky(pred_next), moved_cov), (0, 2, 1))
        * last_keep[:, None, None]
    )
    moved_mean = jnp.einsum("kl,sl->sk", transition, filt_mean, precision=HIGHEST)
    offset = filt_mean - jnp.einsum("skl,sl->sk", gain, moved_mean, precision=HIGHEST)
    resid_cov = filt_cov - jnp.einsum("skl,slm->skm", gain, moved_cov, precision=HIGHEST)
    smooth_identity = (identity_mat, zero_vec, zero_mat)
    local_suffix = lax.associative_scan(smooth_scan_join, (gain, offset, resid_cov), reverse=True)
    smooth_total = jax.tree.map(take_first, local_suffix)
    after = carried_in(smooth_total, "tm", smooth_scan_join, smooth_identity, True)
    smoothed = jax.vmap(smooth_join, in_axes=(0, None))(local_suffix, after)
    smoothed_mean = smoothed[1]
    smoothed_var = jnp.diagonal(smoothed[2], axis1=1, axis2=2)
    return (smoothed_mean, smoothed_var)


def solution(mesh):
    return jax.shard_map(
        per_device,
        mesh=mesh,
        in_specs=(P(("grp", "tm", "unit"), None), P("grp", None), P(), P(), P(), P(), P()),
        out_specs=(P(("grp", "tm"), None), P(("grp", "tm"), None)),
        check_vma=False,
    )
```

profile of v0, /device:TPU:0, one launch (start us, length us, event | category | flops | bytes accessed | tf_op | source)
XLA Modules:
  0.0 1629.7 jit_solution(505296090753852161)
XLA Ops:
  26.4 22.3 %all-reduce.48 = f32[8]{0:T(128)} all-reduce(f32[8]{0:T(128)S(1)} %dynamic-update-slice.10), channel_id=1, replica_groups=mesh['grp'=2,'tm'=8,'unit'=2] {'tm'}, use_global_device_ids=true, to_apply=%add.48 | all-reduce | flops 8 | bytes 64
  59.6 93.8 %custom-call.69 = f32[8,128,128]{2,1,0:T(8,128)S(1)} custom-call(f32[8,128,128]{2,1,0:T(8,128)S(1)} %fusion.120), custom_call_target="Cholesky" | custom-call | tf_op jit(solution)/shard_map/jit(cholesky)/cholesky/custom-call.1 | solution.py:148
  153.8 78.8 %custom-call.71 = f32[8,1,128,128]{2,3,1,0:T(8,128)S(1)} custom-call(f32[8,1,128,128]{3,2,1,0:T(8,128)S(1)} %select_bitcast_fusion.2), custom_call_target="InvertDiagBlocksLowerTriangular" | custom-call | tf_op jit(solution)/shard_map/triangular_solve/custom-call.8 | solution.py:43
  241.8 46.9 %custom-call.72 = f32[4,128,128]{2,1,0:T(8,128)S(1)} custom-call(f32[4,128,128]{2,1,0:T(8,128)S(1)} %fusion.130), custom_call_target="Cholesky" | custom-call | tf_op jit(solution)/shard_map/jit(cholesky)/cholesky | solution.py:51
  292.1 47.1 %custom-call.73 = f32[4,128,128]{2,1,0:T(8,128)S(1)} custom-call(f32[4,128,128]{2,1,0:T(8,128)S(1)} %fusion.129), custom_call_target="Cholesky" | custom-call | tf_op jit(solution)/shard_map/jit(cholesky)/cholesky | solution.py:53
  339.5 39.3 %custom-call.43 = f32[4,1,128,128]{2,3,1,0:T(8,128)S(1)} custom-call(f32[4,1,128,128]{3,2,1,0:T(8,128)S(1)} %fusion.131), custom_call_target="InvertDiagBlocksLowerTriangular" | custom-call | tf_op jit(solution)/shard_map/triangular_solve | solution.py:54
  390.9 23.9 %custom-call.74 = f32[2,128,128]{2,1,0:T(8,128)S(1)} custom-call(f32[2,128,128]{2,1,0:T(8,128)S(1)} %fusion.195), custom_call_target="Cholesky" | custom-call | tf_op jit(solution)/shard_map/jit(cholesky)/cholesky | solution.py:51
  416.0 23.5 %custom-call.75 = f32[2,128,128]{2,1,0:T(8,128)S(1)} custom-call(f32[2,128,128]{2,1,0:T(8,128)S(1)} %fusion.194), custom_call_target="Cholesky" | custom-call | tf_op jit(solution)/shard_map/jit(cholesky)/cholesky | solution.py:53
  439.7 19.8 %custom-call.44 = f32[2,1,128,128]{2,3,1,0:T(8,128)S(1)} custom-call(f32[2,1,128,128]{3,2,1,0:T(8,128)S(1)} %fusion.196), custom_call_target="InvertDiagBlocksLowerTriangular" | custom-call | tf_op jit(solution)/shard_map/triangular_solve | solution.py:54
  565.0 35.2 %custom-call.82 = f32[3,128,128]{2,1,0:T(8,128)S(1)} custom-call(f32[3,128,128]{2,1,0:T(8,128)S(1)} %fusion.178), custom_call_target="Cholesky" | custom-call | tf_op jit(solution)/shard_map/jit(cholesky)/cholesky | solution.py:51
  601.6 35.2 %custom-call.83 = f32[3,128,128]{2,1,0:T(8,128)S(1)} custom-call(f32[3,128,128]{2,1,0:T(8,128)S(1)} %fusion.177), custom_call_target="Cholesky" | custom-call | tf_op jit(solution)/shard_map/jit(cholesky)/cholesky | solution.py:53
  637.1 29.7 %custom-call.45 = f32[3,1,128,128]{2,3,1,0:T(8,128)S(1)} custom-call(f32[3,1,128,128]{3,2,1,0:T(8,128)S(1)} %fusion.179), custom_call_target="InvertDiagBlocksLowerTriangular" | custom-call | tf_op jit(solution)/shard_map/triangular_solve | solution.py:54
  696.6 18.2 %all-gather = f32[8,1,128]{2,1,0:T(1,128)S(1)} all-gather(f32[1,1,128]{2,1,0:T(1,128)S(1)} %slice_bitcast_fusion.20), channel_id=1, replica_groups=mesh['grp'=2,'tm'=8,'unit'=2] {'tm'}, dimensions={0}, use_global_device_ids=true | all-gather | bytes 4608 | tf_op jit(solution)/shard_map/all_gather | solution.py:14
  722.5 33.6 %all_gather.31 = f32[8,128,128]{2,1,0:T(8,128)} all-gather(f32[1,128,128]{2,1,0:T(8,128)S(1)} %copy.470), channel_id=1, replica_groups=mesh['grp'=2,'tm'=8,'unit'=2] {'tm'}, dimensions={0}, use_global_device_ids=true | all-gather | bytes 589824 | tf_op jit(solution)/shard_map/all_gather | solution.py:14
  756.1 33.4 %all_gather.27 = f32[8,128,128]{2,1,0:T(8,128)} all-gather(f32[1,128,128]{2,1,0:T(8,128)S(1)} %slice_add_fusion.6), channel_id=1, replica_groups=mesh['grp'=2,'tm'=8,'unit'=2] {'tm'}, dimensions={0}, use_global_device_ids=true | all-gather | bytes 589824 | tf_op jit(solution)/shard_map/all_gather | solution.py:14
  789.5 33.2 %all_gather.28 = f32[8,128,128]{2,1,0:T(8,128)} all-gather(f32[1,128,128]{2,1,0:T(8,128)S(1)} %slice_add_fusion.5), channel_id=1, replica_groups=mesh['grp'=2,'tm'=8,'unit'=2] {'tm'}, dimensions={0}, use_global_device_ids=true | all-gather | bytes 589824 | tf_op jit(solution)/shard_map/all_gather | solution.py:14
  822.7 317.0 %while.34 = (s32[]{:T(128)}, f32[128]{0:T(128)S(1)}, f32[128,128]{1,0:T(8,128)S(1)}, f32[]{:T(128)}, s32[]{:T(128)}, /*index=5*/f32[8,128,128]{2,1,0:T(8,128)}, ...) while((s32[]{:T(128)}, f32[128]{0:T(128)S(1)}, ...), condition=%wide.region_15.25_spmd.clone, body=%wide.region_12.24_spmd.clone.sunk | while | flops 127288576 | bytes 2435339 | solution.py:26
  1158.0 94.6 %custom-call.85 = f32[8,128,128]{2,1,0:T(8,128)S(1)} custom-call(f32[8,128,128]{2,1,0:T(8,128)} %fusion.115), custom_call_target="Cholesky" | custom-call | tf_op jit(solution)/shard_map/vmap(jit(cholesky))/cholesky/custom-call.1 | solution.py:53
  1252.9 78.8 %custom-call.86 = f32[8,1,128,128]{2,3,1,0:T(8,128)S(1)} custom-call(f32[8,1,128,128]{3,2,1,0:T(8,128)S(1)} %select_bitcast_fusion.1), custom_call_target="InvertDiagBlocksLowerTriangular" | custom-call | tf_op jit(solution)/shard_map/vmap()/triangular_solve/custom-call.7 | solution.py:54
  1340.2 93.8 %custom-call.87 = f32[8,128,128]{2,1,0:T(8,128)S(1)} custom-call(f32[8,128,128]{2,1,0:T(8,128)S(1)} %fusion.108), custom_call_target="Cholesky" | custom-call | tf_op jit(solution)/shard_map/jit(cholesky)/cholesky/custom-call.1 | solution.py:190
  1434.4 78.8 %custom-call.89 = f32[8,1,128,128]{2,3,1,0:T(8,128)S(1)} custom-call(f32[8,1,128,128]{3,2,1,0:T(8,128)S(1)} %select_bitcast_fusion), custom_call_target="InvertDiagBlocksLowerTriangular" | custom-call | tf_op jit(solution)/shard_map/triangular_solve/custom-call.8 | solution.py:43
  1524.9 16.4 %all-gather.2 = f32[8,1,128]{2,1,0:T(1,128)S(1)} all-gather(f32[1,1,128]{2,1,0:T(1,128)S(1)} %slice_bitcast_fusion.18), channel_id=1, replica_groups=mesh['grp'=2,'tm'=8,'unit'=2] {'tm'}, dimensions={0}, use_global_device_ids=true | all-gather | bytes 4608 | tf_op jit(solution)/shard_map/all_gather | solution.py:14
  1541.4 31.3 %all_gather.35 = f32[8,128,128]{2,1,0:T(8,128)S(1)} all-gather(f32[1,128,128]{2,1,0:T(8,128)S(1)} %copy.506), channel_id=1, replica_groups=mesh['grp'=2,'tm'=8,'unit'=2] {'tm'}, dimensions={0}, use_global_device_ids=true | all-gather | bytes 589824 | tf_op jit(solution)/shard_map/all_gather | solution.py:14
  1572.8 31.2 %all_gather.33 = f32[8,128,128]{2,1,0:T(8,128)S(1)} all-gather(f32[1,128,128]{2,1,0:T(8,128)S(1)} %slice_add_fusion.3), channel_id=1, replica_groups=mesh['grp'=2,'tm'=8,'unit'=2] {'tm'}, dimensions={0}, use_global_device_ids=true | all-gather | bytes 589824 | tf_op jit(solution)/shard_map/all_gather | solution.py:14
  (677 shorter events, 573.7 us)
Async XLA Ops:
  7.2 228.6 %copy-start.5 = (f32[128,128]{1,0:T(8,128)S(1)}, f32[128,128]{1,0:T(8,128)}, u32[]{:S(2)}) copy-start(f32[128,128]{1,0:T(8,128)} %param.27) | copy-start | bytes 196612
  8.7 44.8 %all-to-all-start = ((bf16[8,2,128]{2,1,0:T(2,128)(2,1)}), bf16[8,2,128]{2,1,0:T(2,128)(2,1)S(1)}, u32[]{:S(2)}, u32[]{:S(2)}) async-start(bf16[8,2,128]{2,1,0:T(2,128)(2,1)} %reshape.602), calls=%async_computation | async-start | bytes 8192 | tf_op jit(solution)/shard_map/all_to_all | solution.py:125
  16.0 41.0 %all-reduce.51.cloned.1.call-start = ((), (), s32[]{:S(2)}) async-start(), calls=%async_computation.1 | async-start | bytes 1048576 | tf_op jit(solution)/shard_map/psum | solution.py:138
  235.9 145.9 %copy-start.16 = (f32[8,128]{1,0:T(8,128)}, f32[8,128]{1,0:T(8,128)S(1)}, u32[]{:S(2)}) copy-start(f32[8,128]{1,0:T(8,128)S(1)} %convolution_multiply_fusion.3) | copy-start | bytes 12292
  236.2 432.5 %copy-start.3 = (f32[8,128,128]{1,2,0:T(8,128)}, f32[8,128,128]{1,2,0:T(8,128)S(1)}, u32[]{:S(2)}) copy-start(f32[8,128,128]{1,2,0:T(8,128)S(1)} %copy.421) | copy-start | bytes 1572868
  240.4 359.9 %copy-start.2 = (f32[8,128,128]{2,1,0:T(8,128)}, f32[8,128,128]{2,1,0:T(8,128)S(1)}, u32[]{:S(2)}) copy-start(f32[8,128,128]{2,1,0:T(8,128)S(1)} %fusion.76) | copy-start | bytes 1572868
  382.6 148.7 %copy-start.17 = (f32[4,128]{1,0:T(4,128)}, f32[4,128]{1,0:T(4,128)S(1)}, u32[]{:S(2)}) copy-start(f32[4,128]{1,0:T(4,128)S(1)} %subtract_add_fusion) | copy-start | bytes 6148
  386.0 170.7 %copy-start.4 = (f32[4,128,128]{2,1,0:T(8,128)}, f32[4,128,128]{2,1,0:T(8,128)S(1)}, u32[]{:S(2)}) copy-start(f32[4,128,128]{2,1,0:T(8,128)S(1)} %fusion.77) | copy-start | bytes 786436
  460.1 96.9 %copy-start.9 = (f32[4,128,128]{1,2,0:T(8,128)S(1)}, f32[4,128,128]{1,2,0:T(8,128)}, u32[]{:S(2)}) copy-start(f32[4,128,128]{1,2,0:T(8,128)} %copy-done.8) | copy-start | bytes 786436
  460.1 99.3 %slice-start.3 = ((f32[4,128,128]{1,2,0:T(8,128)}), f32[1,128,128]{1,2,0:T(8,128)S(1)}, s32[]{:S(2)}) async-start(f32[4,128,128]{1,2,0:T(8,128)} %copy-done.8), calls=%async_computation.5 | async-start | bytes 131072 | tf_op jit(solution)/shard_map/slice | solution.py:178
  556.9 118.2 %copy-start.21 = (f32[128]{0:T(128)S(1)}, f32[128]{0:T(128)}, u32[]{:S(2)}) copy-start(f32[128]{0:T(128)} %convolution_bitcast_fusion.17) | copy-start | bytes 1540
  557.2 120.1 %slice-start.5 = ((f32[4,128]{1,0:T(4,128)}), f32[1,128]{1,0:T(1,128)S(1)}, s32[]{:S(2)}) async-start(f32[4,128]{1,0:T(4,128)} %copy-done.17), calls=%async_computation.7 | async-start | bytes 1024 | tf_op jit(solution)/shard_map/slice | solution.py:178
  557.2 120.2 %slice-start.2 = ((f32[4,128,128]{2,1,0:T(8,128)}), f32[1,128,128]{2,1,0:T(8,128)S(1)}, s32[]{:S(2)}) async-start(f32[4,128,128]{2,1,0:T(8,128)} %copy-done.4), calls=%async_computation.4 | async-start | bytes 131072 | tf_op jit(solution)/shard_map/slice | solution.py:178
  559.3 115.9 %copy-start.20 = (f32[128,1]{0,1:T(1,128)S(1)}, f32[128,1]{0,1:T(1,128)}, u32[]{:S(2)}) copy-start(f32[128,1]{0,1:T(1,128)} %copy-done.19) | copy-start | bytes 1540
  563.0 116.1 %slice-start.4 = ((f32[8,128]{1,0:T(8,128)}), f32[1,128]{1,0:T(1,128)S(1)}, s32[]{:S(2)}) async-start(f32[8,128]{1,0:T(8,128)} %copy-done.16), calls=%async_computation.6 | async-start | bytes 1024 | tf_op jit(solution)/shard_map/slice | solution.py:178
  600.9 114.0 %slice-start = ((f32[8,128,128]{2,1,0:T(8,128)}), f32[1,128,128]{2,1,0:T(8,128)S(1)}, s32[]{:S(2)}) async-start(f32[8,128,128]{2,1,0:T(8,128)} %copy-done.2), calls=%async_computation.2 | async-start | bytes 131072 | tf_op jit(solution)/shard_map/slice | solution.py:178
  667.9 154.8 %copy-start.24 = (f32[8]{0:T(128)S(1)}, f32[8]{0:T(128)}, u32[]{:S(2)}) copy-start(f32[8]{0:T(128)} %all-reduce.48) | copy-start | bytes 100
  717.8 104.9 %copy-start.6 = (f32[8,128,128]{1,2,0:T(8,128)}, f32[8,128,128]{1,2,0:T(8,128)S(1)}, u32[]{:S(2)}) copy-start(f32[8,128,128]{1,2,0:T(8,128)S(1)} %pad.188) | copy-start | bytes 1572868
  822.7 334.4 %copy-start.14 = (f32[128,128]{1,0:T(8,128)S(1)}, f32[128,128]{1,0:T(8,128)}, u32[]{:S(2)}) copy-start(f32[128,128]{1,0:T(8,128)} %copy.471) | copy-start | bytes 196612
  822.7 334.4 %copy-start.15 = (f32[128,128]{1,0:T(8,128)S(1)}, f32[128,128]{1,0:T(8,128)}, u32[]{:S(2)}) copy-start(f32[128,128]{1,0:T(8,128)} %copy.476) | copy-start | bytes 196612
  1153.6 186.5 %copy-start.12 = (f32[128,128]{1,0:T(8,128)S(1)}, f32[128,128]{1,0:T(8,128)}, u32[]{:S(2)}) copy-start(f32[128,128]{1,0:T(8,128)} %copy.482) | copy-start | bytes 196612
  1153.6 186.5 %copy-start.13 = (f32[128,128]{1,0:T(8,128)S(1)}, f32[128,128]{1,0:T(8,128)}, u32[]{:S(2)}) copy-start(f32[128,128]{1,0:T(8,128)} %copy.484) | copy-start | bytes 196612
  1154.9 180.0 %copy-start.7 = (f32[8,128,128]{1,2,0:T(8,128)S(1)}, f32[8,128,128]{1,2,0:T(8,128)}, u32[]{:S(2)}) copy-start(f32[8,128,128]{1,2,0:T(8,128)} %copy-done.6) | copy-start | bytes 1572868
  1252.6 261.7 %copy-start.23 = (f32[8]{0:T(128)S(1)}, f32[8]{0:T(128)}, u32[]{:S(2)}) copy-start(f32[8]{0:T(128)} %fusion.412) | copy-start | bytes 100
  (9 other events, 289.7 us)
Sparse Core Ops, SparseCore 0:
  21.2 20.1 all-reduce.50
where the time goes:
time: 1640 us; the launch traced here: 1630 us
  other arithmetic  1170 us (71%)
  blocking collectives  238 us (15%)
  matrix products  145 us (9%)
  local copies, waits for them, and re-layouts  43.9 us (3%)
  between operations  16.6 us (1%)
    another operation x39, other arithmetic, filter_join(): inner_factor = jnp.linalg.cholesky(inner_mat)  313 us
    another operation x26, other arithmetic, filter_join(): lax.linalg.triangular_solve(inner_factor, flipped(factor_one), left_side=...  263 us
    another operation x39, other arithmetic, filter_join(): factor_one = jnp.linalg.cholesky(cov_one + (1.0 - live_mat) * identity_mat)  230 us
    all_gather x8, blocking collectives, carried_in(): pieces = jax.tree.map(lambda part: lax.all_gather(part, axis), value)  213 us
    another operation x5, other arithmetic, chol_apply(): lax.linalg.triangular_solve(factor, middle, left_side=True, lower=True, t...  158 us
    another operation x4, other arithmetic, per_device(): jnp.linalg.cholesky(pred_next)  94 us
    another operation x3, other arithmetic, per_device(): post_cov = chol_apply(jnp.linalg.cholesky(prior_prec + info_mat), eyes)  93.9 us
    dot_general x113, matrix products, product(): return jnp.matmul(left, right, precision=HIGHEST)  85 us
  transfers between devices with their start and end apart: 2, of which 0 were waited for; matrix products, arithmetic and copies ran while one was open for 1% of the time, Pallas kernels for 0%

commit v1 on v0

--- a/solution.py
+++ b/solution.py
@@ -1,12 +1,559 @@
+import functools
+
 import jax
 import jax.numpy as jnp
 from jax import lax
+from jax.experimental import pallas as pl
+from jax.experimental.pallas import tpu as pltpu
 from jax.sharding import PartitionSpec as P
 
+f32 = jnp.float32
+bf16 = jnp.bfloat16
+WIDTH = 128
+HIGHEST = lax.Precision.HIGHEST
+VMEM_LIMIT = 30 << 20
+RESIDUAL_MAX = 1e-2
+JOIN_BOUNDS = ((1.0, 3.3), (1.0, 3.0), (1.0, 3.3), (1.0, 4.8), (1.0, 7.2), (1.0, 10.5))
+COV_BOUNDS = ((0.72, 1.32), (0.51, 1.75), (0.31, 2.50), (0.19, 3.75), (0.13, 4.50), (0.09, 5.00))
+
+
+def schedule(bounds, goal=2.5e-3):
+    low, high = bounds
+    alpha, radius, factors = 2.0 / (low + high), (high - low) / (high + low), []
+    while radius > goal:
+        square = radius * radius
+        factors.append(2.0 / (2.0 - square))
+        radius = square / (2.0 - square)
+    return alpha, factors
+
+
+def bounds_at(table, level):
+    return table[min(level, len(table) - 1)]
+
+
+def mm(left, right):
+    return lax.dot_general(left, right, (((1,), (0,)), ((), ())), preferred_element_type=f32)
+
+
+def mm_nt(left, right):
+    return lax.dot_general(left, right, (((1,), (1,)), ((), ())), preferred_element_type=f32)
+
+
+def split(value):
+    high = value.astype(bf16)
+    return high, (value - high.astype(f32)).astype(bf16)
+
+
+def lanes(*parts):
+    return jnp.concatenate(parts, axis=1)
+
+
+def rows(*parts):
+    return jnp.concatenate(parts, axis=0)
+
+
+def mm3(left, right):
+    lh, ll = split(left)
+    rh, rl = split(right)
+    return mm(lanes(lh, ll), rows(rh, rh)) + mm(lh, rl)
+
+
+def mm3_nt(left, right):
+    lh, ll = split(left)
+    rh, rl = split(right)
+    return mm_nt(lanes(lh, ll), lanes(rh, rh)) + mm_nt(lh, rl)
+
+
+def identity():
+    shape = (WIDTH, WIDTH)
+    return (lax.broadcasted_iota(jnp.int32, shape, 0) == lax.broadcasted_iota(jnp.int32, shape, 1)).astype(f32)
+
+
+def squares(value):
+    return jnp.sum((value * value).reshape(WIDTH // 8, 8, WIDTH), axis=0)
+
+
+def fast_inverses(mats, eye, bounds, twice=False):
+    alpha, factors = schedule(bounds)
+    halves = [split(mat) for mat in mats]
+    rest = [eye - alpha * mat for mat in mats]
+    guess = [(alpha * factors[0]) * (eye + r) for r in rest]
+    rest_b = [r.astype(bf16) for r in rest]
+    rest = [(1.0 - factors[0]) * eye + factors[0] * mm(r, r) for r in rest_b]
+    for number, factor in enumerate(factors[1:]):
+        rest_b = [r.astype(bf16) for r in rest]
+        guess_b = [g.astype(bf16) for g in guess]
+        if number == len(factors) - 2:
+            out = [mm(r, g) for r, g in zip(rest_b, guess_b)]
+            guess = [factor * (g + o) for g, o in zip(guess, out)]
+        else:
+            out = [mm(r, lanes(g, r)) for r, g in zip(rest_b, guess_b)]
+            guess = [factor * (g + o[:, :WIDTH]) for g, o in zip(guess, out)]
+            rest = [(1.0 - factor) * eye + factor * o[:, WIDTH:] for o in out]
+    guess_b = [g.astype(bf16) for g in guess]
+    resid = [eye - mm(lanes(h, l), rows(g, g)) for (h, l), g in zip(halves, guess_b)]
+    guess = [g.astype(f32) + mm(g, e.astype(bf16)) for g, e in zip(guess_b, resid)]
+    if twice:
+        resid = [eye - mm3(mat, g) for mat, g in zip(mats, guess)]
+        guess = [g + mm(g.astype(bf16), e.astype(bf16)) for g, e in zip(guess, resid)]
+    return guess, [squares(e) for e in resid]
+
+
+def safe_inverse(mat, eye):
+    size = jnp.max(jnp.sum(jnp.abs(mat), axis=0, keepdims=True), axis=1, keepdims=True)
+    product = functools.partial(jnp.dot, precision=HIGHEST, preferred_element_type=f32)
+
+    def unfinished(state):
+        step, size, _ = state
+        return jnp.logical_and(step < 64, jnp.logical_not(size <= 1e-7))
+
+    def improve(state):
+        step, _, guess = state
+        resid = eye - product(mat, guess)
+        return step + 1, jnp.sum(squares(resid)), guess + product(guess, resid)
+
+    return lax.while_loop(unfinished, improve, (0, f32(jnp.inf), eye / size))[2]
+
+
+def diagonal(mat, eye):
+    return jnp.sum(mat * eye, axis=0, keepdims=True)
+
+
+def scaled(mat, eye):
+    row = 1.0 / diagonal(mat, eye)
+    return mat * row, row
+
+
+def pack(value):
+    return lanes(*split(value))
+
+
+def unpack(value):
+    return value[:, :WIDTH].astype(f32) + value[:, WIDTH:].astype(f32)
+
+
+def path_steps(half, steps, first):
+    found = []
+    for level in reversed(range(half.bit_length() - 1)):
+        stride = 1 << level
+        if 2 * stride > steps:
+            found.append((level, (first // (2 * stride)) * (2 * stride) + stride - 1))
+        else:
+            found += [(level, first + (2 * k + 1) * stride - 1) for k in range(steps // (2 * stride))]
+    return found
+
+
+def up_kernel(steps, index_ref, mask_ref, load_ref, prec_ref, trans_ref, var_ref,
+              uz_ref, yv_ref, gt_ref, cond_ref, shift_ref, weight_ref, end_ref, message_ref,
+              a_ref, c_ref, j_ref, p_ref, gram_ref, base_ref, acc_ref):
+    unit, place, n_unit = index_ref[0], index_ref[1], index_ref[2]
+    half = uz_ref.shape[0]
+    n_levels = half.bit_length() - 1
+    n_blocks = load_ref.shape[0] // WIDTH
+    eye = identity()
+    for block in range(n_blocks):
+        load = load_ref[block * WIDTH:(block + 1) * WIDTH, :]
+        weighted = (jnp.transpose(load.astype(f32)) * prec_ref[block:block + 1, :]).astype(bf16)
+        weight_ref[block] = weighted
+        gram = mm(weighted, load)
+        gram_ref[block] = 0.5 * (gram + jnp.transpose(gram))
+    base_ref[0] = trans_ref[...]
+    base_ref[1] = eye * var_ref[...]
+
+    def info(step):
+        out = jnp.zeros((WIDTH, WIDTH), f32)
+        for block in range(n_blocks):
+            out = out + mask_ref[block, step].astype(f32) * gram_ref[block]
+        return out
+
+    end_ref[...] = info(n_unit * half - 1)
+
+    def leaves(node):
+        step = unit * half + 2 * node
+        start = jnp.where(step == 0, 1.0, 0.0).astype(f32)
+        trans, noise = base_ref[0], base_ref[1]
+        before = info(jnp.maximum(step - 1, 0)) * (1.0 - start)
+        first = (trans * (1.0 - start), noise + start * (eye - noise), before)
+        return first, (trans, noise, info(step))
+
+    def children(level, node):
+        if level == 0:
+            return leaves(node)
+        at = (2 * node + 1) * (1 << level) - 1
+        near = (1 << level) // 2
+        return tuple((a_ref[k], c_ref[k], j_ref[k]) for k in (at - near, at + near))
+
+    def join(level, nodes, fast):
+        pairs = [children(level, node) for node in nodes]
+        mats = [eye + mm3(one[1], two[2]) for one, two in pairs]
+        if fast:
+            inverses, errors = fast_inverses(mats, eye, bounds_at(JOIN_BOUNDS, level))
+            worst = errors[0]
+            for error in errors[1:]:
+                worst = jnp.maximum(worst, error)
+            acc_ref[...] = jnp.maximum(acc_ref[...], worst)
+        else:
+            inverses = [safe_inverse(mat, eye) for mat in mats]
+        us = [mm3(two[0], p) for (one, two), p in zip(pairs, inverses)]
+        vs = [mm3(p, one[0]) for (one, two), p in zip(pairs, inverses)]
+        azs = [mm3(u, lanes(one[0], one[1])) for u, (one, two) in zip(us, pairs)]
+        ys = [mm3(two[2], v) for v, (one, two) in zip(vs, pairs)]
+        cs = [two[1] + mm3_nt(az[:, WIDTH:], two[0]) for az, (one, two) in zip(azs, pairs)]
+        js = [one[2] + mm3(jnp.transpose(one[0]), y) for y, (one, two) in zip(ys, pairs)]
+        for node, p, u, v, az, y, c, j in zip(nodes, inverses, us, vs, azs, ys, cs, js):
+            at = (2 * node + 1) * (1 << level) - 1
+            uh, ul = split(u)
+            zh, zl = split(az[:, WIDTH:])
+            uz_ref[at] = rows(lanes(uh, zh), lanes(ul, zl))
+            yv_ref[at] = rows(pack(y), pack(v))
+            p_ref[at] = p
+            a_ref[at] = az[:, :WIDTH]
+            c_ref[at] = 0.5 * (c + jnp.transpose(c))
+            j_ref[at] = 0.5 * (j + jnp.transpose(j))
+
+    path = path_steps(half, steps, place * steps)
+
+    def condition(entries, fast):
+        level = entries[0][1]
+        mats, scales = zip(*[scaled(c_ref[at], eye) for _, _, at in entries])
+        if fast:
+            inverses, errors = fast_inverses(mats, eye, bounds_at(COV_BOUNDS, level), level > 1)
+            worst = errors[0]
+            for error in errors[1:]:
+                worst = jnp.maximum(worst, error)
+            acc_ref[...] = jnp.maximum(acc_ref[...], worst)
+        else:
+            inverses = [safe_inverse(mat, eye) for mat in mats]
+        for (slot, level, at), inverse, scale in zip(entries, inverses, scales):
+            uz = uz_ref[at]
+            z = uz[:WIDTH, WIDTH:].astype(f32) + uz[WIDTH:, WIDTH:].astype(f32)
+            v = unpack(yv_ref[at, WIDTH:, :])
+            back = mm3(jnp.transpose(inverse) * scale, z)
+            forth = jnp.transpose(back)
+            if level == 0:
+                start = jnp.where(unit * half + at == 0, 1.0, 0.0).astype(f32)
+                first = base_ref[1] + start * (eye - base_ref[1])
+            else:
+                first = c_ref[at - (1 << level) // 2]
+            p = p_ref[at]
+            kept = mm3(p, first)
+            gain = v - mm3(forth, a_ref[at])
+            gt_ref[slot] = pack(rows(jnp.transpose(gain), back))
+            cond = kept - mm3(forth, z)
+            cond_ref[slot] = 0.5 * (cond + jnp.transpose(cond))
+            shift_ref[slot] = pack(rows(jnp.transpose(p), jnp.transpose(kept), -back))
+
+    def sweep(fast):
+        for level in range(n_levels):
+            count = half >> (level + 1)
+            group = min(count, 4) if fast else 1
+
+            def some(block, carry):
+                join(level, [block * group + k for k in range(group)], fast)
+                return carry
+
+            lax.fori_loop(0, count // group, some, 0)
+        entries = [(slot, level, at) for slot, (level, at) in enumerate(path)]
+        for level in reversed(range(n_levels)):
+            some = [entry for entry in entries if entry[1] == level]
+            if fast:
+                condition(some, True)
+            else:
+                for entry in some:
+                    condition([entry], False)
+        top = half // 2 - 1
+        message_ref[0] = a_ref[top]
+        message_ref[1] = c_ref[top]
+        message_ref[2] = j_ref[top]
+
+    acc_ref[...] = jnp.zeros((8, WIDTH), f32)
+    sweep(True)
+    worst = jnp.sum(acc_ref[...])
+
+    @pl.when(jnp.logical_not(worst <= RESIDUAL_MAX))
+    def _():
+        sweep(False)
+
+
+SMEM = pl.BlockSpec(memory_space=pltpu.SMEM)
+VMEM = pl.BlockSpec(memory_space=pltpu.VMEM)
+
+
+def up_sweep(index, cell_mask, loadings, prec_rows, transition, var_row, half, steps):
+    n_blocks = loadings.shape[0] // WIDTH
+    mat = (WIDTH, WIDTH)
+    wide = (2 * WIDTH, 2 * WIDTH)
+    n_path = len(path_steps(half, steps, 0))
+    return pl.pallas_call(
+        functools.partial(up_kernel, steps),
+        out_shape=(
+            jax.ShapeDtypeStruct((half,) + wide, bf16),
+            jax.ShapeDtypeStruct((half,) + wide, bf16),
+            jax.ShapeDtypeStruct((n_path,) + wide, bf16),
+            jax.ShapeDtypeStruct((n_path,) + mat, f32),
+            jax.ShapeDtypeStruct((n_path, 3 * WIDTH, 2 * WIDTH), bf16),
+            jax.ShapeDtypeStruct((n_blocks,) + mat, bf16),
+            jax.ShapeDtypeStruct(mat, f32),
+            jax.ShapeDtypeStruct((3,) + mat, f32),
+        ),
+        in_specs=[SMEM, SMEM] + [VMEM] * 4,
+        out_specs=(VMEM,) * 8,
+        scratch_shapes=[
+            pltpu.VMEM((half,) + mat, f32),
+            pltpu.VMEM((half,) + mat, f32),
+            pltpu.VMEM((half,) + mat, f32),
+            pltpu.VMEM((half,) + mat, f32),
+            pltpu.VMEM((n_blocks,) + mat, f32),
+            pltpu.VMEM((2,) + mat, f32),
+            pltpu.VMEM((8, WIDTH), f32),
+        ],
+        compiler_params=pltpu.CompilerParams(vmem_limit_bytes=VMEM_LIMIT),
+        cost_estimate=pl.CostEstimate(flops=half * 600 * WIDTH**3, transcendentals=0, bytes_accessed=32 << 20),
+        name="up_sweep",
+    )(index, cell_mask, loadings, prec_rows, transition, var_row)
+
+
+def vector_kernel(index_ref, mask_ref, weight_ref, prior_ref, uz_ref, yv_ref, *refs):
+    *pair_refs, leaf_ref, b_ref, e_ref, message_ref, all_ref, panel_ref = refs
+    unit, place = index_ref[0], index_ref[3]
+    half = uz_ref.shape[0]
+    total = panel_ref.shape[1]
+    n_blocks = weight_ref.shape[0]
+    n_time = len(pair_refs)
+    rows_own = pair_refs[0].shape[0] // 2
+    for shift, pair_ref in enumerate(pair_refs):
+        source = lax.rem(place + (n_time - shift), n_time)
+        for k, own in enumerate((unit, 1 - unit)):
+            at = pl.multiple_of((2 * source + own) * rows_own, rows_own)
+            panel_ref[pl.ds(at, rows_own), :] = pair_ref[k * rows_own:(k + 1) * rows_own, :]
+    turned = jnp.zeros((WIDTH, total), f32)
+    for block in range(n_blocks):
+        mask = mask_ref[block:block + 1, :].astype(bf16)
+        turned = turned + mm(weight_ref[block], mask * panel_ref[block * WIDTH:(block + 1) * WIDTH, :])
+    late = pltpu.roll(jnp.transpose(turned), 1, 0)
+    end = late[0:1, :]
+    all_ref[...] = late
+    all_ref[0:1, :] = jnp.zeros((1, WIDTH), f32)
+    leaf_ref[...] = all_ref[pl.ds(pl.multiple_of(unit * half, half), half), :]
+    prior = jnp.where(unit == 0, 1.0, 0.0) * prior_ref[...]
+    zero = jnp.zeros((1, WIDTH), f32)
+    for level in range(half.bit_length() - 1):
+        stride = 1 << level
+        for node in range(half >> (level + 1)):
+            at = (2 * node + 1) * stride - 1
+            if level == 0:
+                b1, b2 = (prior if node == 0 else zero), zero
+                e1, e2 = leaf_ref[at:at + 1, :], leaf_ref[at + 1:at + 2, :]
+            else:
+                one, two = at - stride // 2, at + stride // 2
+                b1, b2 = b_ref[one:one + 1, :], b_ref[two:two + 1, :]
+                e1, e2 = e_ref[one:one + 1, :], e_ref[two:two + 1, :]
+            high, low = split(lanes(b1, e2))
+            out = mm_nt(rows(high, low), uz_ref[at])
+            b_ref[at:at + 1, :] = b2 + out[0:1, :WIDTH] + out[1:2, :WIDTH] + out[0:1, WIDTH:]
+            high, low = split(lanes(-b1, e2))
+            out = mm(rows(high, low), yv_ref[at])
+            e_ref[at:at + 1, :] = e1 + out[0:1, :WIDTH] + out[1:2, :WIDTH] + out[0:1, WIDTH:]
+    top = half // 2 - 1
+    message_ref[...] = rows(b_ref[top:top + 1, :], e_ref[top:top + 1, :], end, jnp.zeros((5, WIDTH), f32))
+
+
+def vector_sweep(index, pairs, cell_mask, weighted, prior_row, uz, yv):
+    total = pairs[0].shape[1]
+    half = uz.shape[0]
+    row = jax.ShapeDtypeStruct((half, WIDTH), f32)
+    return pl.pallas_call(
+        vector_kernel,
+        out_shape=(row, row, row, jax.ShapeDtypeStruct((8, WIDTH), f32)),
+        in_specs=[SMEM] + [VMEM] * (5 + len(pairs)),
+        out_specs=(VMEM,) * 4,
+        scratch_shapes=[
+            pltpu.VMEM((total, WIDTH), f32),
+            pltpu.VMEM((len(pairs) * pairs[0].shape[0], total), bf16),
+        ],
+        compiler_params=pltpu.CompilerParams(vmem_limit_bytes=VMEM_LIMIT),
+        name="vector_sweep",
+    )(index, cell_mask, weighted, prior_row, uz, yv, *pairs)
+
+
+def down_kernel(steps, index_ref, own_ref, other_ref, end_ref, vown_ref, vother_ref, prior_ref, leaf_ref, b_ref, e_ref,
+                gt_ref, cond_ref, shift_ref, out_ref, acc_ref, top_ref):
+    unit, place = index_ref[0], index_ref[1]
+    half = leaf_ref.shape[0]
+    n_levels = half.bit_length() - 1
+    eye = identity()
+    flag = jnp.where(unit == 0, 1.0, 0.0).astype(f32)
+
+    def pick(zero, one):
+        return flag * zero + (1.0 - flag) * one
+
+    cov0 = pick(own_ref[1], other_ref[1])
+    trans1, cov1, info1 = [pick(other_ref[k], own_ref[k]) for k in range(3)]
+    b0 = pick(vown_ref[0:1, :], vother_ref[0:1, :])
+    b1, e1 = [pick(vother_ref[k:k + 1, :], vown_ref[k:k + 1, :]) for k in range(2)]
+    e_end = vown_ref[2:3, :]
+    end = end_ref[...]
+
+    def roots(fast):
+        mat = eye + mm3(cov0, info1)
+        if fast:
+            (p,), (error,) = fast_inverses([mat], eye, bounds_at(JOIN_BOUNDS, n_levels))
+        else:
+            p = safe_inverse(mat, eye)
+        kept = mm3(p, cov0)
+        z = mm3(trans1, kept)
+        cov = cov1 + mm3_nt(z, trans1)
+        cov = 0.5 * (cov + jnp.transpose(cov))
+        mat, scale = scaled(cov, eye)
+        last = eye + mm3(cov, end)
+        if fast:
+            (inverse,), (error2,) = fast_inverses([mat], eye, bounds_at(COV_BOUNDS, n_levels), True)
+            (p_end,), (error3,) = fast_inverses([last], eye, bounds_at(JOIN_BOUNDS, 0))
+            acc_ref[...] = jnp.maximum(error, jnp.maximum(error2, error3))
+        else:
+            inverse = safe_inverse(mat, eye)
+            p_end = safe_inverse(last, eye)
+        top_ref[0], top_ref[1], top_ref[2], top_ref[3] = p, kept, z, cov
+        top_ref[4], top_ref[5] = jnp.transpose(inverse) * scale, p_end
+
+    roots(True)
+    worst = jnp.sum(acc_ref[...])
+
+    @pl.when(jnp.logical_not(worst <= RESIDUAL_MAX))
+    def _():
+        roots(False)
+
+    p, kept, z, cov, inverse, p_end = [top_ref[k] for k in range(6)]
+    back = mm3(inverse, z)
+    forth = jnp.transpose(back)
+    mean_mid = mm3_nt(b0 + mm3(e1, cov0), p)
+    b_end = mm3_nt(mean_mid, trans1) + b1
+    mean_top = mm3_nt(b_end + mm3(e_end, cov), p_end)
+    mean_mid = mean_mid + mm3(mean_top - b_end, back)
+    cov_top = mm3(p_end, cov)
+    cov_top = 0.5 * (cov_top + jnp.transpose(cov_top))
+    cov_cross = mm3(cov_top, back)
+    cov_mid = kept - mm3(forth, z) + mm3(forth, cov_cross)
+    keep = 1.0 - flag
+    joint = rows(
+        lanes(keep * cov_mid, keep * jnp.transpose(cov_cross)),
+        lanes(keep * cov_cross, pick(cov_mid, cov_top)),
+    )
+    means = lanes(keep * mean_mid, pick(mean_mid, mean_top))
+    prior = flag * prior_ref[...]
+    first = place * steps
+    path = path_steps(half, steps, first)
+
+    def shift(slot):
+        level, at = path[slot]
+        row_of = lambda ref, k: ref[pl.ds(k, 1), :]
+        if level == 0:
+            one, two = jnp.where(at == 0, 1.0, 0.0) * prior, row_of(leaf_ref, at + 1)
+        else:
+            near = (1 << level) // 2
+            one, two = row_of(b_ref, at - near), row_of(e_ref, at + near)
+        high, low = split(lanes(one, two, row_of(b_ref, at)))
+        out = mm(rows(high, low), shift_ref[slot])
+        return out[0:1, :WIDTH] + out[1:2, :WIDTH] + out[0:1, WIDTH:]
+
+    shifts = [shift(slot) for slot in range(len(path))]
+
+    def node(slot, joint, means, leaf):
+        packed = gt_ref[slot]
+        gh, gl = packed[:, :WIDTH], packed[:, WIDTH:]
+        jh, jl = split(joint)
+        cross = mm(lanes(jh, jl), rows(gh, gh)) + mm(jh, gl)
+        high, low = split(means)
+        out = mm(rows(high, low), packed)
+        mean = shifts[slot] + out[0:1, :WIDTH] + out[1:2, :WIDTH] + out[0:1, WIDTH:]
+        gain = unpack(packed)
+        if leaf:
+            own = diagonal(cond_ref[slot], eye) + jnp.sum(gain * cross, axis=0, keepdims=True)
+        else:
+            own = cond_ref[slot] + mm3(jnp.transpose(gain), cross)
+        return mean, own, cross
+
+    def left_pair(joint, means, mean, own, cross):
+        c = cross[:WIDTH]
+        return rows(lanes(joint[:WIDTH, :WIDTH], c), lanes(jnp.transpose(c), own)), lanes(means[:, :WIDTH], mean)
+
+    def right_pair(joint, means, mean, own, cross):
+        c = cross[WIDTH:]
+        return rows(lanes(own, jnp.transpose(c)), lanes(c, joint[WIDTH:, WIDTH:])), lanes(mean, means[:, WIDTH:])
+
+    slot = 0
+    while path[slot][0] >= steps.bit_length() - 1:
+        result = node(slot, joint, means, False)
+        go_right = jnp.where(first > path[slot][1], 1.0, 0.0).astype(f32)
+        lj, lm = left_pair(joint, means, *result)
+        rj, rm = right_pair(joint, means, *result)
+        joint = go_right * rj + (1.0 - go_right) * lj
+        means = go_right * rm + (1.0 - go_right) * lm
+        slot += 1
+
+    out_ref[steps - 1:steps, :] = means[:, WIDTH:]
+    out_ref[2 * steps - 1:2 * steps, :] = diagonal(joint[WIDTH:, WIDTH:], eye)
+    todo = [(0, steps, joint, means)]
+    while todo:
+        later = []
+        for low, count, joint, means in todo:
+            stride = count // 2
+            at = low + stride - 1
+            result = node(slot, joint, means, stride == 1)
+            slot += 1
+            out_ref[at:at + 1, :] = result[0]
+            if stride == 1:
+                out_ref[steps + at:steps + at + 1, :] = result[1]
+                continue
+            out_ref[steps + at:steps + at + 1, :] = diagonal(result[1], eye)
+            later.append((low, stride) + left_pair(joint, means, *result))
+            later.append((low + stride, stride) + right_pair(joint, means, *result))
+        todo = later
+
+
+def down_sweep(index, own, other, end, vown, vother, prior_row, leaves, bs, es, gains, conds, shifts, steps):
+    return pl.pallas_call(
+        functools.partial(down_kernel, steps),
+        out_shape=jax.ShapeDtypeStruct((2 * steps, WIDTH), f32),
+        in_specs=[SMEM] + [VMEM] * 12,
+        out_specs=VMEM,
+        scratch_shapes=[pltpu.VMEM((8, WIDTH), f32), pltpu.VMEM((6, WIDTH, WIDTH), f32)],
+        compiler_params=pltpu.CompilerParams(vmem_limit_bytes=VMEM_LIMIT),
+        name="down_sweep",
+    )(index, own, other, end, vown, vother, prior_row, leaves, bs, es, gains, conds, shifts)
+
+
+def redundant(panel_data, cell_mask, loadings, noise_prec, transition, proc_var, prior_mean):
+    n_time = lax.axis_size("tm")
+    n_unit = lax.axis_size("unit")
+    place, unit = lax.axis_index("tm"), lax.axis_index("unit")
+    total = panel_data.shape[1]
+    half = total // n_unit
+    steps = total // n_time
+    per_half = half // steps
+    index = jnp.stack([unit, place % per_half, n_unit, place]).astype(jnp.int32)
+    swap = [(0, 1), (1, 0)]
+    pair = jnp.concatenate([panel_data, lax.ppermute(panel_data, "unit", swap)])
+    transition, pair = lax.optimization_barrier((transition, pair))
+    pairs = [pair] + [
+        lax.ppermute(pair, "tm", [(k, (k + shift) % n_time) for k in range(n_time)]) for shift in range(1, n_time)
+    ]
+    prior_row = prior_mean.reshape(1, WIDTH)
+    uz, yv, gains, conds, shifts, weighted, end, message = up_sweep(
+        index, cell_mask, loadings, noise_prec.reshape(-1, WIDTH), transition, proc_var.reshape(1, WIDTH), half, steps
+    )
+    other = lax.ppermute(message, "unit", swap)
+    leaves, bs, es, vmessage = vector_sweep(index, pairs, cell_mask, weighted, prior_row, uz, yv)
+    vother = lax.ppermute(vmessage, "unit", swap)
+    mine = down_sweep(
+        index, message, other, end, vmessage, vother, prior_row, leaves, bs, es, gains, conds, shifts, steps
+    )
+    theirs = lax.ppermute(mine, "unit", swap)
+    out = jnp.where(unit == place // per_half, mine, theirs)
+    return out[:steps], out[steps:]
+
+
 BLOCK = 128
-
-
-HIGHEST = lax.Precision.HIGHEST
 
 
 def carried_in(value, axis, join, neutral, backward):
@@ -203,9 +750,14 @@
     return (smoothed_mean, smoothed_var)
 
 
+def per_device_any(*arrays):
+    fits = arrays[0].shape[1] <= 64 * lax.axis_size("unit") and lax.axis_size("unit") == 2
+    return redundant(*arrays) if fits else per_device(*arrays)
+
+
 def solution(mesh):
     return jax.shard_map(
-        per_device,
+        per_device_any,
         mesh=mesh,
         in_specs=(P(("grp", "tm", "unit"), None), P("grp", None), P(), P(), P(), P(), P()),
         out_specs=(P(("grp", "tm"), None), P(("grp", "tm"), None)),

time: 1640 us -> 64.1 us (0.04)
  other arithmetic: 1170 us -> 0.78 us
  blocking collectives: 238 us -> 0 us
  matrix products: 145 us -> 0 us
  local copies, waits for them, and re-layouts: 43.9 us -> 4.37 us
  Pallas kernels: 0 us -> 36.3 us
    another operation x116 -> x1, other arithmetic: 1150 us -> 0.08 us  [redundant(): index = jnp.stack([unit, place % per_half, n_unit, place]).astype(jnp.int32)]
    all_gather x8 -> x0, blocking collectives: 213 us -> none  [carried_in(): pieces = jax.tree.map(lambda part: lax.all_gather(part, axis), value)]
    dot_general x201 -> x0, matrix products: 130 us -> none  [the longest x113 85 us: product(): return jnp.matmul(left, right, precision=HIGHEST)]
    pallas_call x0 -> x3, Pallas kernels: none -> 36.3 us  [the longest x1 25.8 us: up_sweep(): pl.pallas_call(functools.partial(up_kernel, steps), out_shape=(jax.ShapeD...]
    unnamed x1 -> x0, blocking collectives: 22.3 us -> none
  transfers between devices with their start and end apart: 2 -> 11, of which waited for: 0 -> 7; matrix products, arithmetic and copies ran while one was open for 1% -> 0% of each run, Pallas kernels for 0% -> 4%
where the time goes in v1:
time: 64.1 us; the launch traced here: 63.8 us
  Pallas kernels  36.3 us (57%)
  starting transfers between devices  13.2 us (21%)
  waiting for transfers between devices  8.51 us (13%)
  local copies, waits for them, and re-layouts  4.37 us (7%)
  other arithmetic  0.78 us (1%)
  between operations  0.67 us (1%)
    pallas_call x1, Pallas kernels, up_sweep(): pl.pallas_call(functools.partial(up_kernel, steps), out_shape=(jax.ShapeD...  25.8 us
    ppermute x7, starting transfers between devices, redundant(): lax.ppermute(pair, 'tm', [(k, (k + shift) % n_time) for k in range(n_time)])  12.1 us
    pallas_call x1, Pallas kernels, down_sweep(): pl.pallas_call(functools.partial(down_kernel, steps), out_shape=jax.Shape...  7.87 us
    ppermute x7, waiting for transfers between devices, redundant(): lax.ppermute(pair, 'tm', [(k, (k + shift) % n_time) for k in range(n_time)])  5.37 us
    unnamed x14, local copies, waits for them, and re-layouts  3.77 us
    pallas_call x1, Pallas kernels, vector_sweep(): pl.pallas_call(vector_kernel, out_shape=(row, row, row, jax.ShapeDtypeStr...  2.64 us
  transfers between devices with their start and end apart: 11, of which 7 were waited for; matrix products, arithmetic and copies ran while one was open for 0% of the time, Pallas kernels for 4%

profile of v1, /device:TPU:0, one launch (start us, length us, event | category | flops | bytes accessed | tf_op | source)
XLA Modules:
  0.0 63.8 jit_solution(8267556415871562982)
XLA Ops:
  0.6 0.5 collective-permute-start
  1.2 1.0 %collective-permute-done = bf16[32,64]{1,0:T(8,128)(2,1)S(1)} collective-permute-done((bf16[32,64]{1,0:T(8,128)(2,1)}, bf16[32,64]{1,0:T(8,128)(2,1)S(1)}, u32[]{:S(2)}, u32[]{:S(2)}) %collective-permute-start) | collective-permute-done | bytes 4128 | tf_op jit(solution)/shard_map/ppermute | solution.py:536
  2.2 0.7 %pad_maximum_fusion.refs_0_ = bf16[64,64]{1,0:T(8,128)(2,1)S(1)} fusion(bf16[32,64]{1,0:T(8,128)(2,1)S(1)} %collective-permute-done, bf16[32,64]{1,0:T(8,128)(2,1)} %param.7), kind=kLoop, calls=%fused_computation | loop fusion | flops 16384 | bytes 16384 | tf_op jit(solution)/shard_map/concatenate | solution.py:536
  2.9 0.7 %copy-done = s32[4,64]{1,0:T(4,128)S(1)} copy-done((s32[4,64]{1,0:T(4,128)S(1)}, s32[4,64]{1,0:T(4,128)}, u32[]{:S(2)}) %copy-start) | copy-done | bytes 1048
  3.6 0.9 %copy-done.3 = bf16[512,128]{1,0:T(8,128)(2,1)S(1)} copy-done((bf16[512,128]{1,0:T(8,128)(2,1)S(1)}, bf16[512,128]{1,0:T(8,128)(2,1)}, u32[]{:S(2)}) %copy-start.3) | copy-done | bytes 131096
  4.5 0.8 %copy-done.4 = f32[128,128]{1,0:T(8,128)S(1)} copy-done((f32[128,128]{1,0:T(8,128)S(1)}, f32[128,128]{1,0:T(8,128)}, u32[]{:S(2)}) %copy-start.4) | copy-done | bytes 65560
  5.3 0.7 %copy-done.5 = f32[512]{0:T(512)S(1)} copy-done((f32[512]{0:T(512)S(1)}, f32[512]{0:T(512)}, u32[]{:S(2)}) %copy-start.5) | copy-done | bytes 2072
  6.0 0.7 %copy-done.6 = f32[128]{0:T(128)S(1)} copy-done((f32[128]{0:T(128)S(1)}, f32[128]{0:T(128)}, u32[]{:S(2)}) %copy-start.6) | copy-done | bytes 536
  6.7 25.8 %up_sweep.1 = (bf16[32,256,256]{2,1,0:T(8,128)(2,1)S(1)}, bf16[32,256,256]{2,1,0:T(8,128)(2,1)S(1)}, bf16[9,256,256]{2,1,0:T(8,128)(2,1)S(1)}, f32[9,128,128]{2,...) custom-call(s32[4]{0:T(128)S(1)} %pad_add_fusion.index_ref, ...), custom_call_target="tpu_custom_call" | custom-call | flops 40265318400 | bytes 33554432 | tf_op jit(solution)/shard_map/up_sweep/pallas_call | solution.py:287
  32.5 0.4 collective-permute-start.1
  32.9 5.7 %collective-permute-start.8 = (bf16[64,64]{1,0:T(8,128)(2,1)S(1)}, bf16[64,64]{1,0:T(8,128)(2,1)S(1)}, u32[]{:S(2)}, u32[]{:S(2)}) collective-permute-start(bf16[64,64]{1,0:T(8,128)(2,1)S(1)} %pad_maximum_fusion.refs_0_), channel_id=1, source_target_pairs={{0,14},{2,0},{4,2},{6,4},{8,6},{10,8},{12,10},{14,12},{1,15},{3,1}... | collective-permute-start | bytes 24584 | tf_op jit(solution)/shard_map/ppermute | solution.py:539
  38.6 0.4 collective-permute-start.7
  39.0 3.0 %collective-permute-start.5 = (bf16[64,64]{1,0:T(8,128)(2,1)S(1)}, bf16[64,64]{1,0:T(8,128)(2,1)S(1)}, u32[]{:S(2)}, u32[]{:S(2)}) collective-permute-start(bf16[64,64]{1,0:T(8,128)(2,1)S(1)} %pad_maximum_fusion.refs_0_), channel_id=1, source_target_pairs={{0,8},{2,10},{4,12},{6,14},{8,0},{10,2},{12,4},{14,6},{1,9},{3,11}... | collective-permute-start | bytes 24584 | tf_op jit(solution)/shard_map/ppermute | solution.py:539
  42.0 0.3 collective-permute-done.7.refs_6_
  42.3 1.6 %collective-permute-start.3 = (bf16[64,64]{1,0:T(8,128)(2,1)S(1)}, bf16[64,64]{1,0:T(8,128)(2,1)S(1)}, u32[]{:S(2)}, u32[]{:S(2)}) collective-permute-start(bf16[64,64]{1,0:T(8,128)(2,1)S(1)} %pad_maximum_fusion.refs_0_), channel_id=1, source_target_pairs={{0,4},{2,6},{4,8},{6,10},{8,12},{10,14},{12,0},{14,2},{1,5},{3,7},... | collective-permute-start | bytes 24584 | tf_op jit(solution)/shard_map/ppermute | solution.py:539
  43.9 1.3 %collective-permute-start.2 = (bf16[64,64]{1,0:T(8,128)(2,1)S(1)}, bf16[64,64]{1,0:T(8,128)(2,1)S(1)}, u32[]{:S(2)}, u32[]{:S(2)}) collective-permute-start(bf16[64,64]{1,0:T(8,128)(2,1)S(1)} %pad_maximum_fusion.refs_0_), channel_id=1, source_target_pairs={{0,2},{2,4},{4,6},{6,8},{8,10},{10,12},{12,14},{14,0},{1,3},{3,5},... | collective-permute-start | bytes 24584 | tf_op jit(solution)/shard_map/ppermute | solution.py:539
  45.2 2.4 %collective-permute-done.4.refs_3_ = bf16[64,64]{1,0:T(8,128)(2,1)S(1)} collective-permute-done((bf16[64,64]{1,0:T(8,128)(2,1)S(1)}, bf16[64,64]{1,0:T(8,128)(2,1)S(1)}, u32[]{:S(2)}, u32[]{:S(2)}) %collective-permute-start.4) | collective-permute-done | bytes 8224 | tf_op jit(solution)/shard_map/ppermute | solution.py:539
  47.6 1.1 %collective-permute-done.3.refs_2_ = bf16[64,64]{1,0:T(8,128)(2,1)S(1)} collective-permute-done((bf16[64,64]{1,0:T(8,128)(2,1)S(1)}, bf16[64,64]{1,0:T(8,128)(2,1)S(1)}, u32[]{:S(2)}, u32[]{:S(2)}) %collective-permute-start.3) | collective-permute-done | bytes 8224 | tf_op jit(solution)/shard_map/ppermute | solution.py:539
  48.7 1.6 %collective-permute-done.2.refs_1_ = bf16[64,64]{1,0:T(8,128)(2,1)S(1)} collective-permute-done((bf16[64,64]{1,0:T(8,128)(2,1)S(1)}, bf16[64,64]{1,0:T(8,128)(2,1)S(1)}, u32[]{:S(2)}, u32[]{:S(2)}) %collective-permute-start.2) | collective-permute-done | bytes 8224 | tf_op jit(solution)/shard_map/ppermute | solution.py:539
  50.3 2.6 %vector_sweep.1 = (f32[32,128]{1,0:T(8,128)S(1)}, f32[32,128]{1,0:T(8,128)S(1)}, f32[32,128]{1,0:T(8,128)S(1)}, f32[8,128]{1,0:T(8,128)S(1)}) custom-call(s32[4]{0:T(128)S(1)} %pad_add_fusion.index_ref, s32[4,64]{1,0:T(4,128)S(1)} %copy-done.1, bf16[4,128,128]{2,1,0:T(8,128)(2,1)S(1)} %get-tuple-element.19.weight_ref, f32[1,128]{1,0:T(1,128)S(1)} %bitcast.6, ...), custom_call_target="tpu_custom_call" | custom-call | tf_op jit(solution)/shard_map/vector_sweep/pallas_call | solution.py:365
  53.0 1.2 %collective-permute-done.9.vother_ref = f32[8,128]{1,0:T(8,128)S(1)} collective-permute-done((f32[8,128]{1,0:T(8,128)S(1)}, f32[8,128]{1,0:T(8,128)S(1)}, u32[]{:S(2)}, u32[]{:S(2)}) %collective-permute-start.9) | collective-permute-done | bytes 4128 | tf_op jit(solution)/shard_map/ppermute | solution.py:547
  54.1 7.9 %down_sweep.1 = f32[16,128]{1,0:T(8,128)S(1)} custom-call(s32[4]{0:T(128)S(1)} %pad_add_fusion.index_ref, f32[3,128,128]{2,1,0:T(8,128)S(1)} %get-tuple-element.17.own_ref, f32[3,128,128]{2,1,0:T(8,128)S(1)} %collective-permute-done.1.other_ref, f32[128,128]{1,0:T(8,128)S(1)} %get-tuple-element.18.end_ref, f32[8,128]{1,0:T(8,128)S(1)} %get-tuple-element.23.vown_ref, ...), custom_call_target="tpu_custom_call" | custom-call | tf_op jit(solution)/shard_map/down_sweep/pallas_call | solution.py:515
  62.2 1.0 %collective-permute-done.10 = f32[16,128]{1,0:T(8,128)S(1)} collective-permute-done((f32[16,128]{1,0:T(8,128)S(1)}, f32[16,128]{1,0:T(8,128)S(1)}, u32[]{:S(2)}, u32[]{:S(2)}) %collective-permute-start.10) | collective-permute-done | bytes 8224 | tf_op jit(solution)/shard_map/ppermute | solution.py:551
  63.2 0.6 fusion
  (19 shorter events, 0.3 us)
Async XLA Ops:
  0.6 1.6 %collective-permute-start = (bf16[32,64]{1,0:T(8,128)(2,1)}, bf16[32,64]{1,0:T(8,128)(2,1)S(1)}, u32[]{:S(2)}, u32[]{:S(2)}) collective-permute-start(bf16[32,64]{1,0:T(8,128)(2,1)} %param.7), channel_id=1, source_target_pairs={{0,1},{1,0},{2,3},{3,2},{4,5},{5,4},{6,7},{7,6},{8,9},{9,8},{10,11... | collective-permute-start | bytes 12296 | tf_op jit(solution)/shard_map/ppermute | solution.py:536
  2.9 0.7 %copy-start = (s32[4,64]{1,0:T(4,128)S(1)}, s32[4,64]{1,0:T(4,128)}, u32[]{:S(2)}) copy-start(s32[4,64]{1,0:T(4,128)} %mask_ref.3) | copy-start | bytes 3076
  3.6 0.9 %copy-start.3 = (bf16[512,128]{1,0:T(8,128)(2,1)S(1)}, bf16[512,128]{1,0:T(8,128)(2,1)}, u32[]{:S(2)}) copy-start(bf16[512,128]{1,0:T(8,128)(2,1)} %load_ref.1) | copy-start | bytes 393220
  4.5 0.8 %copy-start.4 = (f32[128,128]{1,0:T(8,128)S(1)}, f32[128,128]{1,0:T(8,128)}, u32[]{:S(2)}) copy-start(f32[128,128]{1,0:T(8,128)} %trans_ref) | copy-start | bytes 196612
  5.3 0.7 %copy-start.5 = (f32[512]{0:T(512)S(1)}, f32[512]{0:T(512)}, u32[]{:S(2)}) copy-start(f32[512]{0:T(512)} %param.10) | copy-start | bytes 6148
  6.0 0.7 %copy-start.6 = (f32[128]{0:T(128)S(1)}, f32[128]{0:T(128)}, u32[]{:S(2)}) copy-start(f32[128]{0:T(128)} %param.12) | copy-start | bytes 1540
  6.7 43.6 %copy-start.1 = (s32[4,64]{1,0:T(4,128)S(1)}, s32[4,64]{1,0:T(4,128)}, u32[]{:S(2)}) copy-start(s32[4,64]{1,0:T(4,128)} %mask_ref.3) | copy-start | bytes 3076
  6.7 43.6 %copy-start.2 = (f32[128]{0:T(128)S(1)}, f32[128]{0:T(128)}, u32[]{:S(2)}) copy-start(f32[128]{0:T(128)} %param.13) | copy-start | bytes 1540
  32.5 21.7 %collective-permute-start.1 = (f32[3,128,128]{2,1,0:T(8,128)S(1)}, f32[3,128,128]{2,1,0:T(8,128)S(1)}, u32[]{:S(2)}, u32[]{:S(2)}) collective-permute-start(f32[3,128,128]{2,1,0:T(8,128)S(1)} %get-tuple-element.17.own_ref), channel_id=1, source_target_pairs={{0,1},{1,0},{2,3},{3,2},{4,5},{5,4},{6,7},{7,6},{8,9},{9,8},{10,11... | collective-permute-start | bytes 589832 | tf_op jit(solution)/shard_map/ppermute | solution.py:545
  32.9 9.2 %collective-permute-start.8 = (bf16[64,64]{1,0:T(8,128)(2,1)S(1)}, bf16[64,64]{1,0:T(8,128)(2,1)S(1)}, u32[]{:S(2)}, u32[]{:S(2)}) collective-permute-start(bf16[64,64]{1,0:T(8,128)(2,1)S(1)} %pad_maximum_fusion.refs_0_), channel_id=1, source_target_pairs={{0,14},{2,0},{4,2},{6,4},{8,6},{10,8},{12,10},{14,12},{1,15},{3,1}... | collective-permute-start | bytes 24584 | tf_op jit(solution)/shard_map/ppermute | solution.py:539
  38.6 3.7 %collective-permute-start.7 = (bf16[64,64]{1,0:T(8,128)(2,1)S(1)}, bf16[64,64]{1,0:T(8,128)(2,1)S(1)}, u32[]{:S(2)}, u32[]{:S(2)}) collective-permute-start(bf16[64,64]{1,0:T(8,128)(2,1)S(1)} %pad_maximum_fusion.refs_0_), channel_id=1, source_target_pairs={{0,12},{2,14},{4,0},{6,2},{8,4},{10,6},{12,8},{14,10},{1,13},{3,15... | collective-permute-start | bytes 24584 | tf_op jit(solution)/shard_map/ppermute | solution.py:539
  39.0 4.8 %collective-permute-start.6 = (bf16[64,64]{1,0:T(8,128)(2,1)S(1)}, bf16[64,64]{1,0:T(8,128)(2,1)S(1)}, u32[]{:S(2)}, u32[]{:S(2)}) collective-permute-start(bf16[64,64]{1,0:T(8,128)(2,1)S(1)} %pad_maximum_fusion.refs_0_), channel_id=1, source_target_pairs={{0,10},{2,12},{4,14},{6,0},{8,2},{10,4},{12,6},{14,8},{1,11},{3,13... | collective-permute-start | bytes 24584 | tf_op jit(solution)/shard_map/ppermute | solution.py:539
  39.0 6.2 %collective-permute-start.5 = (bf16[64,64]{1,0:T(8,128)(2,1)S(1)}, bf16[64,64]{1,0:T(8,128)(2,1)S(1)}, u32[]{:S(2)}, u32[]{:S(2)}) collective-permute-start(bf16[64,64]{1,0:T(8,128)(2,1)S(1)} %pad_maximum_fusion.refs_0_), channel_id=1, source_target_pairs={{0,8},{2,10},{4,12},{6,14},{8,0},{10,2},{12,4},{14,6},{1,9},{3,11}... | collective-permute-start | bytes 24584 | tf_op jit(solution)/shard_map/ppermute | solution.py:539
  42.0 5.5 %collective-permute-start.4 = (bf16[64,64]{1,0:T(8,128)(2,1)S(1)}, bf16[64,64]{1,0:T(8,128)(2,1)S(1)}, u32[]{:S(2)}, u32[]{:S(2)}) collective-permute-start(bf16[64,64]{1,0:T(8,128)(2,1)S(1)} %pad_maximum_fusion.refs_0_), channel_id=1, source_target_pairs={{0,6},{2,8},{4,10},{6,12},{8,14},{10,0},{12,2},{14,4},{1,7},{3,9},... | collective-permute-start | bytes 24584 | tf_op jit(solution)/shard_map/ppermute | solution.py:539
  42.3 6.4 %collective-permute-start.3 = (bf16[64,64]{1,0:T(8,128)(2,1)S(1)}, bf16[64,64]{1,0:T(8,128)(2,1)S(1)}, u32[]{:S(2)}, u32[]{:S(2)}) collective-permute-start(bf16[64,64]{1,0:T(8,128)(2,1)S(1)} %pad_maximum_fusion.refs_0_), channel_id=1, source_target_pairs={{0,4},{2,6},{4,8},{6,10},{8,12},{10,14},{12,0},{14,2},{1,5},{3,7},... | collective-permute-start | bytes 24584 | tf_op jit(solution)/shard_map/ppermute | solution.py:539
  43.9 6.4 %collective-permute-start.2 = (bf16[64,64]{1,0:T(8,128)(2,1)S(1)}, bf16[64,64]{1,0:T(8,128)(2,1)S(1)}, u32[]{:S(2)}, u32[]{:S(2)}) collective-permute-start(bf16[64,64]{1,0:T(8,128)(2,1)S(1)} %pad_maximum_fusion.refs_0_), channel_id=1, source_target_pairs={{0,2},{2,4},{4,6},{6,8},{8,10},{10,12},{12,14},{14,0},{1,3},{3,5},... | collective-permute-start | bytes 24584 | tf_op jit(solution)/shard_map/ppermute | solution.py:539
  52.9 1.2 %collective-permute-start.9 = (f32[8,128]{1,0:T(8,128)S(1)}, f32[8,128]{1,0:T(8,128)S(1)}, u32[]{:S(2)}, u32[]{:S(2)}) collective-permute-start(f32[8,128]{1,0:T(8,128)S(1)} %get-tuple-element.23.vown_ref), channel_id=1, source_target_pairs={{0,1},{1,0},{2,3},{3,2},{4,5},{5,4},{6,7},{7,6},{8,9},{9,8},{10,11... | collective-permute-start | bytes 12296 | tf_op jit(solution)/shard_map/ppermute | solution.py:547
  62.0 1.2 %collective-permute-start.10 = (f32[16,128]{1,0:T(8,128)S(1)}, f32[16,128]{1,0:T(8,128)S(1)}, u32[]{:S(2)}, u32[]{:S(2)}) collective-permute-start(f32[16,128]{1,0:T(8,128)S(1)} %down_sweep.1), channel_id=1, source_target_pairs={{0,1},{1,0},{2,3},{3,2},{4,5},{5,4},{6,7},{7,6},{8,9},{9,8},{10,11... | collective-permute-start | bytes 24584 | tf_op jit(solution)/shard_map/ppermute | solution.py:551

commit v2 on v1

--- a/solution.py
+++ b/solution.py
@@ -13,6 +13,7 @@
 HIGHEST = lax.Precision.HIGHEST
 VMEM_LIMIT = 30 << 20
 RESIDUAL_MAX = 1e-2
+GROUP = 8
 JOIN_BOUNDS = ((1.0, 3.3), (1.0, 3.0), (1.0, 3.3), (1.0, 4.8), (1.0, 7.2), (1.0, 10.5))
 COV_BOUNDS = ((0.72, 1.32), (0.51, 1.75), (0.31, 2.50), (0.19, 3.75), (0.13, 4.50), (0.09, 5.00))
 
@@ -73,30 +74,43 @@
     return jnp.sum((value * value).reshape(WIDTH // 8, 8, WIDTH), axis=0)
 
 
-def fast_inverses(mats, eye, bounds, twice=False):
-    alpha, factors = schedule(bounds)
+def fast_inverses(items, eye):
+    mats = [mat for mat, _, _ in items]
+    plans = [schedule(bounds) for _, bounds, _ in items]
+    n = range(len(items))
     halves = [split(mat) for mat in mats]
-    rest = [eye - alpha * mat for mat in mats]
-    guess = [(alpha * factors[0]) * (eye + r) for r in rest]
-    rest_b = [r.astype(bf16) for r in rest]
-    rest = [(1.0 - factors[0]) * eye + factors[0] * mm(r, r) for r in rest_b]
-    for number, factor in enumerate(factors[1:]):
+    rest = [eye - plan[0] * mat for plan, mat in zip(plans, mats)]
+    guess = [(plan[0] * plan[1][0]) * (eye + r) for plan, r in zip(plans, rest)]
+    for step in range(max(len(factors) for _, factors in plans)):
         rest_b = [r.astype(bf16) for r in rest]
         guess_b = [g.astype(bf16) for g in guess]
-        if number == len(factors) - 2:
-            out = [mm(r, g) for r, g in zip(rest_b, guess_b)]
-            guess = [factor * (g + o) for g, o in zip(guess, out)]
-        else:
-            out = [mm(r, lanes(g, r)) for r, g in zip(rest_b, guess_b)]
-            guess = [factor * (g + o[:, :WIDTH]) for g, o in zip(guess, out)]
-            rest = [(1.0 - factor) * eye + factor * o[:, WIDTH:] for o in out]
+        for k in n:
+            factors = plans[k][1]
+            more = step + 1 < len(factors)
+            if step >= len(factors):
+                continue
+            factor = factors[step]
+            if step == 0:
+                if more:
+                    rest[k] = (1.0 - factor) * eye + factor * mm(rest_b[k], rest_b[k])
+            elif more:
+                out = mm(rest_b[k], lanes(guess_b[k], rest_b[k]))
+                guess[k] = factor * (guess[k] + out[:, :WIDTH])
+                rest[k] = (1.0 - factor) * eye + factor * out[:, WIDTH:]
+            else:
+                guess[k] = factor * (guess[k] + mm(rest_b[k], guess_b[k]))
     guess_b = [g.astype(bf16) for g in guess]
     resid = [eye - mm(lanes(h, l), rows(g, g)) for (h, l), g in zip(halves, guess_b)]
     guess = [g.astype(f32) + mm(g, e.astype(bf16)) for g, e in zip(guess_b, resid)]
-    if twice:
-        resid = [eye - mm3(mat, g) for mat, g in zip(mats, guess)]
-        guess = [g + mm(g.astype(bf16), e.astype(bf16)) for g, e in zip(guess, resid)]
-    return guess, [squares(e) for e in resid]
+    again = [k for k in n if items[k][2]]
+    fine = {k: eye - mm3(mats[k], guess[k]) for k in again}
+    for k in again:
+        resid[k] = fine[k]
+        guess[k] = guess[k] + mm(guess[k].astype(bf16), fine[k].astype(bf16))
+    worst = squares(resid[0])
+    for e in resid[1:]:
+        worst = jnp.maximum(worst, squares(e))
+    return guess, worst
 
 
 def safe_inverse(mat, eye):
@@ -143,26 +157,99 @@
     return found
 
 
-def up_kernel(steps, index_ref, mask_ref, load_ref, prec_ref, trans_ref, var_ref,
-              uz_ref, yv_ref, gt_ref, cond_ref, shift_ref, weight_ref, end_ref, message_ref,
-              a_ref, c_ref, j_ref, p_ref, gram_ref, base_ref, acc_ref):
-    unit, place, n_unit = index_ref[0], index_ref[1], index_ref[2]
-    half = uz_ref.shape[0]
-    n_levels = half.bit_length() - 1
+def join_item(level, pair, eye):
+    (_, c1, _), (_, _, j2) = pair
+    return eye + mm3(c1, j2), bounds_at(JOIN_BOUNDS, level), False
+
+
+def joined(level, pairs, inverses, eye, turned=None):
+    if level < 2:
+        less = [(eye - p).astype(bf16) for p in inverses]
+        us = [two[0] - mm(two[0].astype(bf16), d) for (one, two), d in zip(pairs, less)]
+        vs = [one[0] - mm(d, one[0].astype(bf16)) for (one, two), d in zip(pairs, less)]
+    else:
+        us = [mm3(two[0], p) for (one, two), p in zip(pairs, inverses)]
+        vs = [mm3(p, one[0]) for (one, two), p in zip(pairs, inverses)]
+    if turned is None:
+        turned = [jnp.transpose(one[0]) for one, two in pairs]
+    ts = [mm3(two[0], v) for v, (one, two) in zip(vs, pairs)]
+    zs = [mm3(u, one[1]) for u, (one, two) in zip(us, pairs)]
+    ys = [mm3(two[2], v) for v, (one, two) in zip(vs, pairs)]
+    cs = [two[1] + mm3_nt(z, two[0]) for z, (one, two) in zip(zs, pairs)]
+    js = [one[2] + mm3(t, y) for t, y, (one, two) in zip(turned, ys, pairs)]
+    return list(zip(us, vs, ts, zs, ys, cs, js))
+
+
+def condition_item(level, entry, eye):
+    mat, scale = scaled(entry["c"], eye)
+    return (mat, bounds_at(COV_BOUNDS, level), level > 2), scale
+
+
+def conditioned(entries, scales, inverses):
+    zs, vs = [e["z"] for e in entries], [e["v"] for e in entries]
+    backs = [mm3(jnp.transpose(inverse) * scale, z) for inverse, scale, z in zip(inverses, scales, zs)]
+    kepts = [mm3(e["p"], e["c1"]) for e in entries]
+    forths = [jnp.transpose(back) for back in backs]
+    gains = [v - mm3(forth, e["a"]) for v, forth, e in zip(vs, forths, entries)]
+    conds = [kept - mm3(forth, z) for kept, forth, z in zip(kepts, forths, zs)]
+    return [
+        (
+            pack(rows(jnp.transpose(gain), back)),
+            cond,
+            pack(rows(jnp.transpose(e["p"]), jnp.transpose(kept), -back)),
+        )
+        for e, gain, back, cond, kept in zip(entries, gains, backs, conds, kepts)
+    ]
+
+
+def level_entry(refs, level, node, c1):
+    uz_ref, yv_ref, a_ref, c_ref, _, p_ref = refs
+    uz = uz_ref[node]
+    return dict(
+        z=uz[:WIDTH, WIDTH:].astype(f32) + uz[WIDTH:, WIDTH:].astype(f32),
+        v=unpack(yv_ref[node, WIDTH:, :]),
+        a=a_ref[node],
+        c=c_ref[node],
+        p=p_ref[node],
+        c1=c1,
+    )
+
+
+LEVEL_ARRAYS = 6
+
+
+def first_kernel(half, index_ref, mask_hbm, load_hbm, prec_hbm, trans_hbm, var_hbm, prior_hbm,
+                 weight_ref, end_ref, mask_out, const_ref, uz_ref, yv_ref, a_ref, c_ref, j_ref, p_ref,
+                 gram_ref, acc_ref, mask_ref, mask_vmem, load_ref, prec_ref, base_ref, row_ref, sems):
+    unit, n_unit = index_ref[0], index_ref[2]
+    copies = [
+        pltpu.make_async_copy(source, target, sems.at[k])
+        for k, (source, target) in enumerate((
+            (load_hbm, load_ref), (prec_hbm, prec_ref), (trans_hbm, base_ref.at[0]), (var_hbm, row_ref.at[0]),
+            (prior_hbm, row_ref.at[1]), (mask_hbm, mask_ref), (mask_hbm, mask_vmem),
+        ))
+    ]
+    for copy in copies:
+        copy.start()
+    for copy in copies:
+        copy.wait()
+    eye = identity()
     n_blocks = load_ref.shape[0] // WIDTH
-    eye = identity()
     for block in range(n_blocks):
         load = load_ref[block * WIDTH:(block + 1) * WIDTH, :]
         weighted = (jnp.transpose(load.astype(f32)) * prec_ref[block:block + 1, :]).astype(bf16)
         weight_ref[block] = weighted
         gram = mm(weighted, load)
         gram_ref[block] = 0.5 * (gram + jnp.transpose(gram))
-    base_ref[0] = trans_ref[...]
-    base_ref[1] = eye * var_ref[...]
+    base_ref[1] = eye * row_ref[0]
+    base_ref[2] = jnp.transpose(base_ref[0])
+    const_ref[0] = jnp.broadcast_to(row_ref[1], (WIDTH, WIDTH))
+    const_ref[1] = base_ref[1]
+    mask_out[...] = mask_vmem[...].astype(f32).astype(bf16)
 
     def info(step):
-        out = jnp.zeros((WIDTH, WIDTH), f32)
-        for block in range(n_blocks):
+        out = mask_ref[0, step].astype(f32) * gram_ref[0]
+        for block in range(1, n_blocks):
             out = out + mask_ref[block, step].astype(f32) * gram_ref[block]
         return out
 
@@ -176,96 +263,34 @@
         first = (trans * (1.0 - start), noise + start * (eye - noise), before)
         return first, (trans, noise, info(step))
 
-    def children(level, node):
-        if level == 0:
-            return leaves(node)
-        at = (2 * node + 1) * (1 << level) - 1
-        near = (1 << level) // 2
-        return tuple((a_ref[k], c_ref[k], j_ref[k]) for k in (at - near, at + near))
-
-    def join(level, nodes, fast):
-        pairs = [children(level, node) for node in nodes]
-        mats = [eye + mm3(one[1], two[2]) for one, two in pairs]
-        if fast:
-            inverses, errors = fast_inverses(mats, eye, bounds_at(JOIN_BOUNDS, level))
-            worst = errors[0]
-            for error in errors[1:]:
-                worst = jnp.maximum(worst, error)
-            acc_ref[...] = jnp.maximum(acc_ref[...], worst)
-        else:
-            inverses = [safe_inverse(mat, eye) for mat in mats]
-        us = [mm3(two[0], p) for (one, two), p in zip(pairs, inverses)]
-        vs = [mm3(p, one[0]) for (one, two), p in zip(pairs, inverses)]
-        azs = [mm3(u, lanes(one[0], one[1])) for u, (one, two) in zip(us, pairs)]
-        ys = [mm3(two[2], v) for v, (one, two) in zip(vs, pairs)]
-        cs = [two[1] + mm3_nt(az[:, WIDTH:], two[0]) for az, (one, two) in zip(azs, pairs)]
-        js = [one[2] + mm3(jnp.transpose(one[0]), y) for y, (one, two) in zip(ys, pairs)]
-        for node, p, u, v, az, y, c, j in zip(nodes, inverses, us, vs, azs, ys, cs, js):
-            at = (2 * node + 1) * (1 << level) - 1
-            uh, ul = split(u)
-            zh, zl = split(az[:, WIDTH:])
-            uz_ref[at] = rows(lanes(uh, zh), lanes(ul, zl))
-            yv_ref[at] = rows(pack(y), pack(v))
-            p_ref[at] = p
-            a_ref[at] = az[:, :WIDTH]
-            c_ref[at] = 0.5 * (c + jnp.transpose(c))
-            j_ref[at] = 0.5 * (j + jnp.transpose(j))
-
-    path = path_steps(half, steps, place * steps)
-
-    def condition(entries, fast):
-        level = entries[0][1]
-        mats, scales = zip(*[scaled(c_ref[at], eye) for _, _, at in entries])
-        if fast:
-            inverses, errors = fast_inverses(mats, eye, bounds_at(COV_BOUNDS, level), level > 1)
-            worst = errors[0]
-            for error in errors[1:]:
-                worst = jnp.maximum(worst, error)
-            acc_ref[...] = jnp.maximum(acc_ref[...], worst)
-        else:
-            inverses = [safe_inverse(mat, eye) for mat in mats]
-        for (slot, level, at), inverse, scale in zip(entries, inverses, scales):
-            uz = uz_ref[at]
-            z = uz[:WIDTH, WIDTH:].astype(f32) + uz[WIDTH:, WIDTH:].astype(f32)
-            v = unpack(yv_ref[at, WIDTH:, :])
-            back = mm3(jnp.transpose(inverse) * scale, z)
-            forth = jnp.transpose(back)
-            if level == 0:
-                start = jnp.where(unit * half + at == 0, 1.0, 0.0).astype(f32)
-                first = base_ref[1] + start * (eye - base_ref[1])
-            else:
-                first = c_ref[at - (1 << level) // 2]
-            p = p_ref[at]
-            kept = mm3(p, first)
-            gain = v - mm3(forth, a_ref[at])
-            gt_ref[slot] = pack(rows(jnp.transpose(gain), back))
-            cond = kept - mm3(forth, z)
-            cond_ref[slot] = 0.5 * (cond + jnp.transpose(cond))
-            shift_ref[slot] = pack(rows(jnp.transpose(p), jnp.transpose(kept), -back))
+    outs = (uz_ref, yv_ref, a_ref, c_ref, j_ref, p_ref)
 
     def sweep(fast):
-        for level in range(n_levels):
-            count = half >> (level + 1)
-            group = min(count, 4) if fast else 1
-
-            def some(block, carry):
-                join(level, [block * group + k for k in range(group)], fast)
-                return carry
-
-            lax.fori_loop(0, count // group, some, 0)
-        entries = [(slot, level, at) for slot, (level, at) in enumerate(path)]
-        for level in reversed(range(n_levels)):
-            some = [entry for entry in entries if entry[1] == level]
-            if fast:
-                condition(some, True)
-            else:
-                for entry in some:
-                    condition([entry], False)
-        top = half // 2 - 1
-        message_ref[0] = a_ref[top]
-        message_ref[1] = c_ref[top]
-        message_ref[2] = j_ref[top]
-
+        count = half // 2
+        group = min(count, GROUP) if fast else 1
+
+        def some(block, carry):
+            nodes = [block * group + k for k in range(group)]
+            pairs = [leaves(node) for node in nodes]
+            items = [join_item(0, pair, eye) for pair in pairs]
+            inverses = invert(items, eye, fast, acc_ref)
+            store_joined(outs, nodes, inverses, joined(0, pairs, inverses, eye, [base_ref[2]] * group))
+            return carry
+
+        lax.fori_loop(0, count // group, some, 0)
+
+    checked(sweep, acc_ref)
+
+
+def invert(items, eye, fast, acc_ref):
+    if not fast:
+        return [safe_inverse(mat, eye) for mat, _, _ in items]
+    inverses, worst = fast_inverses(items, eye)
+    acc_ref[...] = jnp.maximum(acc_ref[...], worst)
+    return inverses
+
+
+def checked(sweep, acc_ref):
     acc_ref[...] = jnp.zeros((8, WIDTH), f32)
     sweep(True)
     worst = jnp.sum(acc_ref[...])
@@ -275,70 +300,217 @@
         sweep(False)
 
 
+def store_joined(outs, nodes, inverses, results):
+    uz_ref, yv_ref, a_ref, c_ref, j_ref, p_ref = outs
+    for node, p, (u, v, t, z, y, c, j) in zip(nodes, inverses, results):
+        uh, ul = split(u)
+        zh, zl = split(z)
+        uz_ref[node] = rows(lanes(uh, zh), lanes(ul, zl))
+        yv_ref[node] = rows(pack(y), pack(v))
+        p_ref[node] = p
+        a_ref[node] = t
+        c_ref[node] = c
+        j_ref[node] = j
+
+
+def entries_of(level, half, steps, first, unit, refs, below):
+    found = []
+    for at_level, at in path_steps(half, steps, first):
+        if at_level != level:
+            continue
+        node = at // (2 << level)
+        if level == 0:
+            eye = identity()
+            start = jnp.where(unit * half + at == 0, 1.0, 0.0).astype(f32)
+            c1 = below + start * (eye - below)
+        else:
+            c1 = below[2 * node]
+        found.append(level_entry(refs, level, node, c1))
+    return found
+
+
+def up_kernel(joins, half, steps, index_ref, const_ref, *refs):
+    unit, place = index_ref[0], index_ref[1]
+    low = joins[0]
+    held = {}
+    refs = list(refs)
+    if low > 1:
+        below_ref = refs.pop(0)
+    held[low - 1], refs = refs[:LEVEL_ARRAYS], refs[LEVEL_ARRAYS:]
+    outs = {}
+    for level in joins:
+        held[level], refs = refs[:LEVEL_ARRAYS], refs[LEVEL_ARRAYS:]
+        outs[level], refs = refs[:3], refs[3:]
+    acc_ref, = refs
+    eye = identity()
+
+    def children(level, node):
+        _, _, a_ref, c_ref, j_ref, _ = held[level - 1]
+        return tuple((a_ref[k], c_ref[k], j_ref[k]) for k in (2 * node, 2 * node + 1))
+
+    def condition_inputs(level):
+        if level == 0:
+            below = const_ref[1]
+        elif level == low - 1:
+            below = below_ref
+        else:
+            below = held[level - 1][3]
+        return entries_of(level, half, steps, place * steps, unit, held[level], below)
+
+    def store(level, results):
+        for slot, result in enumerate(results):
+            for ref, value in zip(outs[level], result):
+                ref[slot] = value
+
+    def sweep(fast):
+        for level in joins:
+            count = half >> (level + 1)
+            under = level - 1
+            if fast and count <= GROUP:
+                nodes = list(range(count))
+                entries = condition_inputs(under)
+                pairs = [children(level, node) for node in nodes]
+                items = [join_item(level, pair, eye) for pair in pairs]
+                extra = [condition_item(under, entry, eye) for entry in entries]
+                inverses = invert(items + [item for item, _ in extra], eye, True, acc_ref)
+                store_joined(held[level], nodes, inverses[:count], joined(level, pairs, inverses[:count], eye))
+                store(level, conditioned(entries, [scale for _, scale in extra], inverses[count:]))
+                continue
+            group = min(count, GROUP) if fast else 1
+
+            def some(block, carry):
+                nodes = [block * group + k for k in range(group)]
+                pairs = [children(level, node) for node in nodes]
+                inverses = invert([join_item(level, pair, eye) for pair in pairs], eye, fast, acc_ref)
+                store_joined(held[level], nodes, inverses, joined(level, pairs, inverses, eye))
+                return carry
+
+            lax.fori_loop(0, count // group, some, 0)
+            entries = condition_inputs(under)
+            extra = [condition_item(under, entry, eye) for entry in entries]
+            inverses = invert([item for item, _ in extra], eye, fast, acc_ref)
+            store(level, conditioned(entries, [scale for _, scale in extra], inverses))
+
+    checked(sweep, acc_ref)
+
+
 SMEM = pl.BlockSpec(memory_space=pltpu.SMEM)
 VMEM = pl.BlockSpec(memory_space=pltpu.VMEM)
 
 
-def up_sweep(index, cell_mask, loadings, prec_rows, transition, var_row, half, steps):
+ANY = pl.BlockSpec(memory_space=pl.ANY)
+
+
+def level_shapes(half, level):
+    count = half >> (level + 1)
+    mat = (count, WIDTH, WIDTH)
+    wide = (count, 2 * WIDTH, 2 * WIDTH)
+    return [jax.ShapeDtypeStruct(wide, bf16)] * 2 + [jax.ShapeDtypeStruct(mat, f32)] * 4
+
+
+def path_shapes(half, steps, level):
+    count = len([k for k, _ in path_steps(half, steps, 0) if k == level])
+    return [
+        jax.ShapeDtypeStruct((count, 2 * WIDTH, 2 * WIDTH), bf16),
+        jax.ShapeDtypeStruct((count, WIDTH, WIDTH), f32),
+        jax.ShapeDtypeStruct((count, 3 * WIDTH, 2 * WIDTH), bf16),
+    ]
+
+
+def estimate(matrices):
+    return pl.CostEstimate(flops=matrices * 600 * WIDTH**3, transcendentals=0, bytes_accessed=1 << 20)
+
+
+def first_sweep(half, index, cell_mask, loadings, prec_rows, transition, var_row, prior_row):
+    mat = (WIDTH, WIDTH)
     n_blocks = loadings.shape[0] // WIDTH
-    mat = (WIDTH, WIDTH)
-    wide = (2 * WIDTH, 2 * WIDTH)
-    n_path = len(path_steps(half, steps, 0))
+    outs = [
+        jax.ShapeDtypeStruct((n_blocks,) + mat, bf16),
+        jax.ShapeDtypeStruct(mat, f32),
+        jax.ShapeDtypeStruct(cell_mask.shape, bf16),
+        jax.ShapeDtypeStruct((2,) + mat, f32),
+    ] + level_shapes(half, 0)
+    inputs = [
+        pltpu.with_memory_space_constraint(array, pltpu.HBM)
+        for array in (cell_mask, loadings, prec_rows, transition, var_row, prior_row)
+    ]
     return pl.pallas_call(
-        functools.partial(up_kernel, steps),
-        out_shape=(
-            jax.ShapeDtypeStruct((half,) + wide, bf16),
-            jax.ShapeDtypeStruct((half,) + wide, bf16),
-            jax.ShapeDtypeStruct((n_path,) + wide, bf16),
-            jax.ShapeDtypeStruct((n_path,) + mat, f32),
-            jax.ShapeDtypeStruct((n_path, 3 * WIDTH, 2 * WIDTH), bf16),
-            jax.ShapeDtypeStruct((n_blocks,) + mat, bf16),
-            jax.ShapeDtypeStruct(mat, f32),
-            jax.ShapeDtypeStruct((3,) + mat, f32),
-        ),
-        in_specs=[SMEM, SMEM] + [VMEM] * 4,
-        out_specs=(VMEM,) * 8,
+        functools.partial(first_kernel, half),
+        out_shape=outs,
+        in_specs=[SMEM] + [ANY] * 6,
+        out_specs=[VMEM] * len(outs),
         scratch_shapes=[
-            pltpu.VMEM((half,) + mat, f32),
-            pltpu.VMEM((half,) + mat, f32),
-            pltpu.VMEM((half,) + mat, f32),
-            pltpu.VMEM((half,) + mat, f32),
             pltpu.VMEM((n_blocks,) + mat, f32),
-            pltpu.VMEM((2,) + mat, f32),
             pltpu.VMEM((8, WIDTH), f32),
+            pltpu.SMEM(cell_mask.shape, jnp.int32),
+            pltpu.VMEM(cell_mask.shape, jnp.int32),
+            pltpu.VMEM(loadings.shape, bf16),
+            pltpu.VMEM(prec_rows.shape, f32),
+            pltpu.VMEM((3,) + mat, f32),
+            pltpu.VMEM((2, 1, WIDTH), f32),
+            pltpu.SemaphoreType.DMA((7,)),
         ],
         compiler_params=pltpu.CompilerParams(vmem_limit_bytes=VMEM_LIMIT),
-        cost_estimate=pl.CostEstimate(flops=half * 600 * WIDTH**3, transcendentals=0, bytes_accessed=32 << 20),
-        name="up_sweep",
-    )(index, cell_mask, loadings, prec_rows, transition, var_row)
-
-
-def vector_kernel(index_ref, mask_ref, weight_ref, prior_ref, uz_ref, yv_ref, *refs):
+        cost_estimate=estimate(half // 2),
+        name="first_sweep",
+    )(index, *inputs)
+
+
+def up_sweep(joins, half, steps, index, consts, held):
+    low = joins[0]
+    operands = ([held[low - 2][3]] if low > 1 else []) + list(held[low - 1])
+    outs = []
+    for level in joins:
+        outs += level_shapes(half, level) + path_shapes(half, steps, level - 1)
+    results = pl.pallas_call(
+        functools.partial(up_kernel, joins, half, steps),
+        out_shape=outs,
+        in_specs=[SMEM] + [VMEM] * (1 + len(operands)),
+        out_specs=[VMEM] * len(outs),
+        scratch_shapes=[pltpu.VMEM((8, WIDTH), f32)],
+        compiler_params=pltpu.CompilerParams(vmem_limit_bytes=VMEM_LIMIT),
+        cost_estimate=estimate(sum(half >> level for level in joins)),
+        name="up_sweep_%d" % low,
+    )(index, consts, *operands)
+    results = list(results)
+    step = LEVEL_ARRAYS + 3
+    parts = [results[k * step:(k + 1) * step] for k in range(len(joins))]
+    return [part[:LEVEL_ARRAYS] for part in parts], [part[LEVEL_ARRAYS:] for part in parts]
+
+
+def vector_kernel(half, rows_own, index_ref, mask_ref, weight_ref, const_ref, *refs):
+    n_levels = half.bit_length() - 1
+    gain_refs, refs = refs[:2 * n_levels], refs[2 * n_levels:]
     *pair_refs, leaf_ref, b_ref, e_ref, message_ref, all_ref, panel_ref = refs
     unit, place = index_ref[0], index_ref[3]
-    half = uz_ref.shape[0]
     total = panel_ref.shape[1]
     n_blocks = weight_ref.shape[0]
-    n_time = len(pair_refs)
-    rows_own = pair_refs[0].shape[0] // 2
-    for shift, pair_ref in enumerate(pair_refs):
-        source = lax.rem(place + (n_time - shift), n_time)
-        for k, own in enumerate((unit, 1 - unit)):
-            at = pl.multiple_of((2 * source + own) * rows_own, rows_own)
-            panel_ref[pl.ds(at, rows_own), :] = pair_ref[k * rows_own:(k + 1) * rows_own, :]
+    panel_in, = pair_refs
+    n_time = panel_in.shape[0] // (2 * rows_own)
+    for k in range(panel_in.shape[0] // rows_own):
+        core, chip, hop = unit, place, n_time // 2
+        for bit in range(n_time.bit_length() - 1):
+            if (k >> bit) % 2:
+                chip = jnp.bitwise_xor(chip, hop)
+            hop = hop // 2
+        if k >= n_time:
+            core = 1 - unit
+        at = pl.multiple_of((2 * chip + core) * rows_own, rows_own)
+        panel_ref[pl.ds(at, rows_own), :] = panel_in[k * rows_own:(k + 1) * rows_own, :]
     turned = jnp.zeros((WIDTH, total), f32)
     for block in range(n_blocks):
-        mask = mask_ref[block:block + 1, :].astype(bf16)
+        mask = mask_ref[block:block + 1, :]
         turned = turned + mm(weight_ref[block], mask * panel_ref[block * WIDTH:(block + 1) * WIDTH, :])
     late = pltpu.roll(jnp.transpose(turned), 1, 0)
     end = late[0:1, :]
     all_ref[...] = late
     all_ref[0:1, :] = jnp.zeros((1, WIDTH), f32)
     leaf_ref[...] = all_ref[pl.ds(pl.multiple_of(unit * half, half), half), :]
-    prior = jnp.where(unit == 0, 1.0, 0.0) * prior_ref[...]
+    prior = jnp.where(unit == 0, 1.0, 0.0) * const_ref[0, 0:1, :]
     zero = jnp.zeros((1, WIDTH), f32)
     for level in range(half.bit_length() - 1):
         stride = 1 << level
+        uz_ref, yv_ref = gain_refs[2 * level:2 * level + 2]
         for node in range(half >> (level + 1)):
             at = (2 * node + 1) * stride - 1
             if level == 0:
@@ -349,23 +521,22 @@
                 b1, b2 = b_ref[one:one + 1, :], b_ref[two:two + 1, :]
                 e1, e2 = e_ref[one:one + 1, :], e_ref[two:two + 1, :]
             high, low = split(lanes(b1, e2))
-            out = mm_nt(rows(high, low), uz_ref[at])
+            out = mm_nt(rows(high, low), uz_ref[node])
             b_ref[at:at + 1, :] = b2 + out[0:1, :WIDTH] + out[1:2, :WIDTH] + out[0:1, WIDTH:]
             high, low = split(lanes(-b1, e2))
-            out = mm(rows(high, low), yv_ref[at])
+            out = mm(rows(high, low), yv_ref[node])
             e_ref[at:at + 1, :] = e1 + out[0:1, :WIDTH] + out[1:2, :WIDTH] + out[0:1, WIDTH:]
     top = half // 2 - 1
     message_ref[...] = rows(b_ref[top:top + 1, :], e_ref[top:top + 1, :], end, jnp.zeros((5, WIDTH), f32))
 
 
-def vector_sweep(index, pairs, cell_mask, weighted, prior_row, uz, yv):
+def vector_sweep(half, rows_own, index, mask, weighted, consts, gains, pairs):
     total = pairs[0].shape[1]
-    half = uz.shape[0]
     row = jax.ShapeDtypeStruct((half, WIDTH), f32)
     return pl.pallas_call(
-        vector_kernel,
+        functools.partial(vector_kernel, half, rows_own),
         out_shape=(row, row, row, jax.ShapeDtypeStruct((8, WIDTH), f32)),
-        in_specs=[SMEM] + [VMEM] * (5 + len(pairs)),
+        in_specs=[SMEM] + [VMEM] * (3 + len(gains) + len(pairs)),
         out_specs=(VMEM,) * 4,
         scratch_shapes=[
             pltpu.VMEM((total, WIDTH), f32),
@@ -373,11 +544,15 @@
         ],
         compiler_params=pltpu.CompilerParams(vmem_limit_bytes=VMEM_LIMIT),
         name="vector_sweep",
-    )(index, cell_mask, weighted, prior_row, uz, yv, *pairs)
-
-
-def down_kernel(steps, index_ref, own_ref, other_ref, end_ref, vown_ref, vother_ref, prior_ref, leaf_ref, b_ref, e_ref,
-                gt_ref, cond_ref, shift_ref, out_ref, acc_ref, top_ref):
+    )(index, mask, weighted, consts, *gains, *pairs)
+
+
+def down_kernel(steps, index_ref, own_ref, other_ref, end_ref, vown_ref, vother_ref, const_ref, leaf_ref, b_ref, e_ref, below_ref,
+                *refs):
+    refs = list(refs)
+    top_refs, refs = refs[:LEVEL_ARRAYS], refs[LEVEL_ARRAYS:]
+    out_ref, acc_ref, top_ref, gt_ref, cond_ref, shift_ref = refs[-6:]
+    path_refs = refs[:-6]
     unit, place = index_ref[0], index_ref[1]
     half = leaf_ref.shape[0]
     n_levels = half.bit_length() - 1
@@ -394,35 +569,29 @@
     e_end = vown_ref[2:3, :]
     end = end_ref[...]
 
+    first = place * steps
+
     def roots(fast):
-        mat = eye + mm3(cov0, info1)
-        if fast:
-            (p,), (error,) = fast_inverses([mat], eye, bounds_at(JOIN_BOUNDS, n_levels))
-        else:
-            p = safe_inverse(mat, eye)
+        under = n_levels - 1
+        entries = entries_of(under, half, steps, first, unit, top_refs, below_ref)
+        extra = [condition_item(under, entry, eye) for entry in entries]
+        item = (eye + mm3(cov0, info1), bounds_at(JOIN_BOUNDS, n_levels), False)
+        p, *inverses = invert([item] + [item for item, _ in extra], eye, fast, acc_ref)
         kept = mm3(p, cov0)
         z = mm3(trans1, kept)
         cov = cov1 + mm3_nt(z, trans1)
         cov = 0.5 * (cov + jnp.transpose(cov))
         mat, scale = scaled(cov, eye)
-        last = eye + mm3(cov, end)
-        if fast:
-            (inverse,), (error2,) = fast_inverses([mat], eye, bounds_at(COV_BOUNDS, n_levels), True)
-            (p_end,), (error3,) = fast_inverses([last], eye, bounds_at(JOIN_BOUNDS, 0))
-            acc_ref[...] = jnp.maximum(error, jnp.maximum(error2, error3))
-        else:
-            inverse = safe_inverse(mat, eye)
-            p_end = safe_inverse(last, eye)
+        results = conditioned(entries, [scale for _, scale in extra], inverses)
+        for slot, result in enumerate(results):
+            for ref, value in zip((gt_ref, cond_ref, shift_ref), result):
+                ref[slot] = value
+        last = (eye + mm3(cov, end), bounds_at(JOIN_BOUNDS, 0), False)
+        inverse, p_end = invert([(mat, bounds_at(COV_BOUNDS, n_levels), True), last], eye, fast, acc_ref)
         top_ref[0], top_ref[1], top_ref[2], top_ref[3] = p, kept, z, cov
         top_ref[4], top_ref[5] = jnp.transpose(inverse) * scale, p_end
 
-    roots(True)
-    worst = jnp.sum(acc_ref[...])
-
-    @pl.when(jnp.logical_not(worst <= RESIDUAL_MAX))
-    def _():
-        roots(False)
-
+    checked(roots, acc_ref)
     p, kept, z, cov, inverse, p_end = [top_ref[k] for k in range(6)]
     back = mm3(inverse, z)
     forth = jnp.transpose(back)
@@ -440,9 +609,13 @@
         lanes(keep * cov_cross, pick(cov_mid, cov_top)),
     )
     means = lanes(keep * mean_mid, pick(mean_mid, mean_top))
-    prior = flag * prior_ref[...]
-    first = place * steps
+    prior = flag * const_ref[0, 0:1, :]
     path = path_steps(half, steps, first)
+    levels = [(gt_ref, cond_ref, shift_ref)] + [path_refs[k:k + 3] for k in range(0, len(path_refs), 3)]
+    places, seen = [], {}
+    for level, _ in path:
+        seen[level] = seen.get(level, -1) + 1
+        places.append((levels[n_levels - 1 - level], seen[level]))
 
     def shift(slot):
         level, at = path[slot]
@@ -453,13 +626,15 @@
             near = (1 << level) // 2
             one, two = row_of(b_ref, at - near), row_of(e_ref, at + near)
         high, low = split(lanes(one, two, row_of(b_ref, at)))
-        out = mm(rows(high, low), shift_ref[slot])
+        arrays, own = places[slot]
+        out = mm(rows(high, low), arrays[2][own])
         return out[0:1, :WIDTH] + out[1:2, :WIDTH] + out[0:1, WIDTH:]
 
     shifts = [shift(slot) for slot in range(len(path))]
 
     def node(slot, joint, means, leaf):
-        packed = gt_ref[slot]
+        (gt_ref, cond_ref, _), at = places[slot]
+        packed = gt_ref[at]
         gh, gl = packed[:, :WIDTH], packed[:, WIDTH:]
         jh, jl = split(joint)
         cross = mm(lanes(jh, jl), rows(gh, gh)) + mm(jh, gl)
@@ -468,9 +643,9 @@
         mean = shifts[slot] + out[0:1, :WIDTH] + out[1:2, :WIDTH] + out[0:1, WIDTH:]
         gain = unpack(packed)
         if leaf:
-            own = diagonal(cond_ref[slot], eye) + jnp.sum(gain * cross, axis=0, keepdims=True)
+            own = diagonal(cond_ref[at], eye) + jnp.sum(gain * cross, axis=0, keepdims=True)
         else:
-            own = cond_ref[slot] + mm3(jnp.transpose(gain), cross)
+            own = cond_ref[at] + mm3(jnp.transpose(gain), cross)
         return mean, own, cross
 
     def left_pair(joint, means, mean, own, cross):
@@ -511,16 +686,17 @@
         todo = later
 
 
-def down_sweep(index, own, other, end, vown, vother, prior_row, leaves, bs, es, gains, conds, shifts, steps):
+def down_sweep(steps, half, *operands):
     return pl.pallas_call(
         functools.partial(down_kernel, steps),
         out_shape=jax.ShapeDtypeStruct((2 * steps, WIDTH), f32),
-        in_specs=[SMEM] + [VMEM] * 12,
+        in_specs=[SMEM] + [VMEM] * (len(operands) - 1),
         out_specs=VMEM,
-        scratch_shapes=[pltpu.VMEM((8, WIDTH), f32), pltpu.VMEM((6, WIDTH, WIDTH), f32)],
+        scratch_shapes=[pltpu.VMEM((8, WIDTH), f32), pltpu.VMEM((6, WIDTH, WIDTH), f32)]
+        + [pltpu.VMEM(shape.shape, shape.dtype) for shape in path_shapes(half, steps, half.bit_length() - 2)],
         compiler_params=pltpu.CompilerParams(vmem_limit_bytes=VMEM_LIMIT),
         name="down_sweep",
-    )(index, own, other, end, vown, vother, prior_row, leaves, bs, es, gains, conds, shifts)
+    )(*operands)
 
 
 def redundant(panel_data, cell_mask, loadings, noise_prec, transition, proc_var, prior_mean):
@@ -533,20 +709,38 @@
     per_half = half // steps
     index = jnp.stack([unit, place % per_half, n_unit, place]).astype(jnp.int32)
     swap = [(0, 1), (1, 0)]
-    pair = jnp.concatenate([panel_data, lax.ppermute(panel_data, "unit", swap)])
-    transition, pair = lax.optimization_barrier((transition, pair))
-    pairs = [pair] + [
-        lax.ppermute(pair, "tm", [(k, (k + shift) % n_time) for k in range(n_time)]) for shift in range(1, n_time)
-    ]
-    prior_row = prior_mean.reshape(1, WIDTH)
-    uz, yv, gains, conds, shifts, weighted, end, message = up_sweep(
-        index, cell_mask, loadings, noise_prec.reshape(-1, WIDTH), transition, proc_var.reshape(1, WIDTH), half, steps
-    )
+
+    def swapped(value, other):
+        return lax.ppermute(value, "tm", [(k, k ^ other) for k in range(n_time)])
+
+    n_levels = half.bit_length() - 1
+    hops = [1 << k for k in reversed(range(n_time.bit_length() - 1))]
+    weighted, end, mask, consts, *level0 = first_sweep(
+        half, index, cell_mask, loadings, noise_prec.reshape(-1, WIDTH), transition,
+        proc_var.reshape(1, WIDTH), prior_mean.reshape(1, WIDTH),
+    )
+    held, paths = [level0], []
+    panel = panel_data
+    cuts = [[1], [2], list(range(3, n_levels))]
+    panel = jnp.concatenate([panel, swapped(panel, hops[0])])
+    for k, joins in enumerate(cuts):
+        panel, latest = lax.optimization_barrier((panel, held[-1]))
+        held[-1] = latest
+        if k + 1 < len(hops):
+            panel = jnp.concatenate([panel, swapped(panel, hops[k + 1])])
+        else:
+            panel = jnp.concatenate([panel, lax.ppermute(panel, "unit", swap)])
+        new, path = up_sweep(joins, half, steps, index, consts, held)
+        held += new
+        paths += path
+    message = jnp.concatenate(held[-1][2:5])
     other = lax.ppermute(message, "unit", swap)
-    leaves, bs, es, vmessage = vector_sweep(index, pairs, cell_mask, weighted, prior_row, uz, yv)
+    gains = [array for level in held for array in level[:2]]
+    leaves, bs, es, vmessage = vector_sweep(half, panel_data.shape[0], index, mask, weighted, consts, gains, [panel])
     vother = lax.ppermute(vmessage, "unit", swap)
     mine = down_sweep(
-        index, message, other, end, vmessage, vother, prior_row, leaves, bs, es, gains, conds, shifts, steps
+        steps, half, index, message, other, end, vmessage, vother, consts, leaves, bs, es, held[-2][3], *held[-1],
+        *[array for path in reversed(paths) for array in path],
     )
     theirs = lax.ppermute(mine, "unit", swap)
     out = jnp.where(unit == place // per_half, mine, theirs)

time: 64.1 us -> 43.5 us (0.68)
  Pallas kernels: 36.3 us -> 30.5 us
  waiting for transfers between devices: 8.51 us -> 2.92 us
  starting transfers between devices: 13.2 us -> 8.4 us
  local copies, waits for them, and re-layouts: 4.37 us -> 0.62 us
    pallas_call x2 -> x5, Pallas kernels: 28.4 us -> 22.4 us  [the longest x3 12.3 us: up_sweep(): pl.pallas_call(functools.partial(up_kernel, joins, half, steps), out_shap...]
    ppermute x8 -> x4, waiting for transfers between devices: 6.33 us -> 1.03 us  [the longest x1 1.02 us: redundant(): panel = jnp.concatenate([panel, lax.ppermute(panel, 'unit', swap)])]
    ppermute x8 -> x4, starting transfers between devices: 12.6 us -> 7.8 us  [the longest x3 7.3 us: swapped(): return lax.ppermute(value, 'tm', [(k, k ^ other) for k in range(n_time)])]
    unnamed x14 -> x4, local copies, waits for them, and re-layouts: 3.77 us -> 0.01 us
  transfers between devices with their start and end apart: 11 -> 7, of which waited for: 7 -> 3; matrix products, arithmetic and copies ran while one was open for 0% -> 0% of each run, Pallas kernels for 4% -> 39%
where the time goes in v2:
time: 43.5 us; the launch traced here: 43.3 us
  Pallas kernels  30.5 us (70%)
  starting transfers between devices  8.4 us (19%)
  waiting for transfers between devices  2.92 us (7%)
  between operations  0.74 us (2%)
  local copies, waits for them, and re-layouts  0.62 us (1%)
    pallas_call x3, Pallas kernels, up_sweep(): pl.pallas_call(functools.partial(up_kernel, joins, half, steps), out_shap...  12.3 us
    pallas_call x1, Pallas kernels, down_sweep(): pl.pallas_call(functools.partial(down_kernel, steps), out_shape=jax.Shape...  8.07 us
    pallas_call x1, Pallas kernels, first_sweep(): pl.pallas_call(functools.partial(first_kernel, half), out_shape=outs, in_...  7.48 us
    ppermute x3, starting transfers between devices, swapped(): return lax.ppermute(value, 'tm', [(k, k ^ other) for k in range(n_time)])  7.3 us
    pallas_call x1, Pallas kernels, vector_sweep(): pl.pallas_call(functools.partial(vector_kernel, half, rows_own), out_shap...  2.65 us
    ppermute x1, waiting for transfers between devices, redundant(): panel = jnp.concatenate([panel, lax.ppermute(panel, 'unit', swap)])  1.02 us
    ppermute x1, waiting for transfers between devices, redundant(): theirs = lax.ppermute(mine, 'unit', swap)  0.95 us
    ppermute x1, waiting for transfers between devices, redundant(): vother = lax.ppermute(vmessage, 'unit', swap)  0.94 us
  transfers between devices with their start and end apart: 7, of which 3 were waited for; matrix products, arithmetic and copies ran while one was open for 0% of the time, Pallas kernels for 39%

profile of v2, /device:TPU:0, one launch (start us, length us, event | category | flops | bytes accessed | tf_op | source)
XLA Modules:
  0.0 43.3 jit_solution(13084034840137191650)
XLA Ops:
  0.6 4.1 %collective-permute-start = (bf16[32,64]{1,0:T(8,128)(2,1)}, bf16[32,64]{1,0:T(8,128)(2,1)S(1)}, u32[]{:S(2)}, u32[]{:S(2)}) collective-permute-start(bf16[32,64]{1,0:T(8,128)(2,1)} %param.7), channel_id=1, source_target_pairs={{0,8},{2,10},{4,12},{6,14},{8,0},{10,2},{12,4},{14,6},{1,9},{3,11}... | collective-permute-start | bytes 12296 | tf_op jit(solution)/shard_map/ppermute | solution.py:714
  4.7 0.1 pad_add_fusion.index_ref
  4.8 0.0 copy-start
  4.8 7.5 %first_sweep.1 = (bf16[4,128,128]{2,1,0:T(8,128)(2,1)S(1)}, f32[128,128]{1,0:T(8,128)S(1)}, bf16[4,64]{1,0:T(4,128)(2,1)S(1)}, f32[2,128,128]{2,1,0:T(8,128)S(1)...) custom-call(s32[4]{0:T(128)S(1)} %pad_add_fusion.index_ref, ...), custom_call_target="tpu_custom_call" | custom-call | flops 20132659200 | bytes 1048576 | tf_op jit(solution)/shard_map/first_sweep/pallas_call | solution.py:437
  12.3 0.0 collective-permute-done
  12.3 0.0 copy-done
  12.3 1.6 %collective-permute-start.1 = (bf16[64,64]{1,0:T(8,128)(2,1)S(1)}, bf16[64,64]{1,0:T(8,128)(2,1)S(1)}, u32[]{:S(2)}, u32[]{:S(2)}) collective-permute-start(bf16[64,64]{1,0:T(8,128)(2,1)S(1)} %pad_maximum_fusion.3), channel_id=1, source_target_pairs={{0,4},{2,6},{4,0},{6,2},{8,12},{10,14},{12,8},{14,10},{1,5},{3,7},... | collective-permute-start | bytes 24584 | tf_op jit(solution)/shard_map/ppermute | solution.py:714
  14.0 3.8 %up_sweep_1.1 = (bf16[8,256,256]{2,1,0:T(8,128)(2,1)S(1)}, bf16[8,256,256]{2,1,0:T(8,128)(2,1)S(1)}, f32[8,128,128]{2,1,0:T(8,128)S(1)}, f32[8,128,128]{2,1,0:T(...) custom-call(s32[4]{0:T(128)S(1)} %pad_add_fusion.index_ref, ...), custom_call_target="tpu_custom_call" | custom-call | flops 20132659200 | bytes 1048576 | tf_op jit(solution)/shard_map/up_sweep_1/pallas_call | solution.py:465
  17.8 0.0 collective-permute-done.1
  17.8 1.6 %collective-permute-start.2 = (bf16[128,64]{1,0:T(8,128)(2,1)S(1)}, bf16[128,64]{1,0:T(8,128)(2,1)S(1)}, u32[]{:S(2)}, u32[]{:S(2)}) collective-permute-start(bf16[128,64]{1,0:T(8,128)(2,1)S(1)} %pad_maximum_fusion.2), channel_id=1, source_target_pairs={{0,2},{2,0},{4,6},{6,4},{8,10},{10,8},{12,14},{14,12},{1,3},{3,1},... | collective-permute-start | bytes 49160 | tf_op jit(solution)/shard_map/ppermute | solution.py:714
  19.4 3.1 %up_sweep_2.1 = (bf16[4,256,256]{2,1,0:T(8,128)(2,1)S(1)}, bf16[4,256,256]{2,1,0:T(8,128)(2,1)S(1)}, f32[4,128,128]{2,1,0:T(8,128)S(1)}, f32[4,128,128]{2,1,0:T(...) custom-call(s32[4]{0:T(128)S(1)} %pad_add_fusion.index_ref, ...), custom_call_target="tpu_custom_call" | custom-call | flops 10066329600 | bytes 1048576 | tf_op jit(solution)/shard_map/up_sweep_2/pallas_call | solution.py:465
  22.5 0.0 collective-permute-done.2
  22.5 5.3 %up_sweep_3.1 = (bf16[2,256,256]{2,1,0:T(8,128)(2,1)S(1)}, bf16[2,256,256]{2,1,0:T(8,128)(2,1)S(1)}, f32[2,128,128]{2,1,0:T(8,128)}, f32[2,128,128]{2,1,0:T(8,12...) custom-call(s32[4]{0:T(128)S(1)} %pad_add_fusion.index_ref, ...), custom_call_target="tpu_custom_call" | custom-call | flops 7549747200 | bytes 1048576 | tf_op jit(solution)/shard_map/up_sweep_3/pallas_call | solution.py:465
  27.9 0.1 collective-permute-start.3
  28.0 0.5 %collective-permute-start.4 = (bf16[256,64]{1,0:T(8,128)(2,1)S(1)}, bf16[256,64]{1,0:T(8,128)(2,1)S(1)}, u32[]{:S(2)}, u32[]{:S(2)}) collective-permute-start(bf16[256,64]{1,0:T(8,128)(2,1)S(1)} %pad_maximum_fusion.1), channel_id=1, source_target_pairs={{0,1},{1,0},{2,3},{3,2},{4,5},{5,4},{6,7},{7,6},{8,9},{9,8},{10,11... | collective-permute-start | bytes 98312 | tf_op jit(solution)/shard_map/ppermute | solution.py:732
  28.5 1.0 %collective-permute-done.4 = bf16[256,64]{1,0:T(8,128)(2,1)S(1)} collective-permute-done((bf16[256,64]{1,0:T(8,128)(2,1)S(1)}, bf16[256,64]{1,0:T(8,128)(2,1)S(1)}, u32[]{:S(2)}, u32[]{:S(2)}) %collective-permute-start.4) | collective-permute-done | bytes 32800 | tf_op jit(solution)/shard_map/ppermute | solution.py:732
  29.6 2.6 %vector_sweep.1 = (f32[32,128]{1,0:T(8,128)S(1)}, f32[32,128]{1,0:T(8,128)S(1)}, f32[32,128]{1,0:T(8,128)S(1)}, f32[8,128]{1,0:T(8,128)S(1)}) custom-call(s32[4]{0:T(128)S(1)} %pad_add_fusion.index_ref, bf16[4,64]{1,0:T(4,128)(2,1)S(1)} %get-tuple-element.113.mask_ref, bf16[4,128,128]{2,1,0:T(8,128)(2,1)S(1)} %get-tuple-element.114.weight_ref, ...), custom_call_target="tpu_custom_call" | custom-call | tf_op jit(solution)/shard_map/vector_sweep/pallas_call | solution.py:536
  32.2 0.2 collective-permute-start.5
  32.4 0.9 %collective-permute-done.5.vother_ref = f32[8,128]{1,0:T(8,128)S(1)} collective-permute-done((f32[8,128]{1,0:T(8,128)S(1)}, f32[8,128]{1,0:T(8,128)S(1)}, u32[]{:S(2)}, u32[]{:S(2)}) %collective-permute-start.5) | collective-permute-done | bytes 4128 | tf_op jit(solution)/shard_map/ppermute | solution.py:740
  33.4 0.0 collective-permute-done.3.other_ref
  33.4 8.1 %down_sweep.1 = f32[16,128]{1,0:T(8,128)S(1)} custom-call(s32[4]{0:T(128)S(1)} %pad_add_fusion.index_ref, f32[3,128,128]{2,1,0:T(8,128)S(1)} %constant_dynamic-update-slice_fusion.own_ref, f32[3,128,128]{2,1,0:T(8,128)S(1)} %collective-permute-done.3.other_ref, f32[128,128]{1,0:T(8,128)S(1)} %get-tuple-element.112.end_ref, ...), custom_call_target="tpu_custom_call" | custom-call | tf_op jit(solution)/shard_map/down_sweep/pallas_call | solution.py:690
  41.5 0.3 collective-permute-start.6
  41.7 0.9 %collective-permute-done.6 = f32[16,128]{1,0:T(8,128)S(1)} collective-permute-done((f32[16,128]{1,0:T(8,128)S(1)}, f32[16,128]{1,0:T(8,128)S(1)}, u32[]{:S(2)}, u32[]{:S(2)}) %collective-permute-start.6) | collective-permute-done | bytes 8224 | tf_op jit(solution)/shard_map/ppermute | solution.py:745
  42.7 0.6 %fusion = (f32[8,128]{1,0:T(8,128)}, f32[8,128]{1,0:T(8,128)}) fusion(f32[16,128]{1,0:T(8,128)S(1)} %broadcast_select_fusion), kind=kLoop, calls=%fused_computation.9 | loop fusion | bytes 16384 | tf_op jit(solution)/shard_map/slice | solution.py:747
  (8 shorter events, 0.1 us)
Async XLA Ops:
  0.6 11.7 %collective-permute-start = (bf16[32,64]{1,0:T(8,128)(2,1)}, bf16[32,64]{1,0:T(8,128)(2,1)S(1)}, u32[]{:S(2)}, u32[]{:S(2)}) collective-permute-start(bf16[32,64]{1,0:T(8,128)(2,1)} %param.7), channel_id=1, source_target_pairs={{0,8},{2,10},{4,12},{6,14},{8,0},{10,2},{12,4},{14,6},{1,9},{3,11}... | collective-permute-start | bytes 12296 | tf_op jit(solution)/shard_map/ppermute | solution.py:714
  4.8 7.5 %copy-start = (bf16[32,64]{1,0:T(8,128)(2,1)S(1)}, bf16[32,64]{1,0:T(8,128)(2,1)}, u32[]{:S(2)}) copy-start(bf16[32,64]{1,0:T(8,128)(2,1)} %param.7) | copy-start | bytes 12292
  12.3 5.5 %collective-permute-start.1 = (bf16[64,64]{1,0:T(8,128)(2,1)S(1)}, bf16[64,64]{1,0:T(8,128)(2,1)S(1)}, u32[]{:S(2)}, u32[]{:S(2)}) collective-permute-start(bf16[64,64]{1,0:T(8,128)(2,1)S(1)} %pad_maximum_fusion.3), channel_id=1, source_target_pairs={{0,4},{2,6},{4,0},{6,2},{8,12},{10,14},{12,8},{14,10},{1,5},{3,7},... | collective-permute-start | bytes 24584 | tf_op jit(solution)/shard_map/ppermute | solution.py:714
  17.8 4.7 %collective-permute-start.2 = (bf16[128,64]{1,0:T(8,128)(2,1)S(1)}, bf16[128,64]{1,0:T(8,128)(2,1)S(1)}, u32[]{:S(2)}, u32[]{:S(2)}) collective-permute-start(bf16[128,64]{1,0:T(8,128)(2,1)S(1)} %pad_maximum_fusion.2), channel_id=1, source_target_pairs={{0,2},{2,0},{4,6},{6,4},{8,10},{10,8},{12,14},{14,12},{1,3},{3,1},... | collective-permute-start | bytes 49160 | tf_op jit(solution)/shard_map/ppermute | solution.py:714
  27.9 5.5 %collective-permute-start.3 = (f32[3,128,128]{2,1,0:T(8,128)S(1)}, f32[3,128,128]{2,1,0:T(8,128)S(1)}, u32[]{:S(2)}, u32[]{:S(2)}) collective-permute-start(f32[3,128,128]{2,1,0:T(8,128)S(1)} %constant_dynamic-update-slice_fusion.own_ref), channel_id=1, source_target_pairs={{0,1},{1,0},{2,3},{3,2},{4,5},{5,4},{6,7},{7,6},{8,9},{9,8},{10,11... | collective-permute-start | bytes 589832 | tf_op jit(solution)/shard_map/ppermute | solution.py:737
  28.0 1.5 %collective-permute-start.4 = (bf16[256,64]{1,0:T(8,128)(2,1)S(1)}, bf16[256,64]{1,0:T(8,128)(2,1)S(1)}, u32[]{:S(2)}, u32[]{:S(2)}) collective-permute-start(bf16[256,64]{1,0:T(8,128)(2,1)S(1)} %pad_maximum_fusion.1), channel_id=1, source_target_pairs={{0,1},{1,0},{2,3},{3,2},{4,5},{5,4},{6,7},{7,6},{8,9},{9,8},{10,11... | collective-permute-start | bytes 98312 | tf_op jit(solution)/shard_map/ppermute | solution.py:732
  32.2 1.2 %collective-permute-start.5 = (f32[8,128]{1,0:T(8,128)S(1)}, f32[8,128]{1,0:T(8,128)S(1)}, u32[]{:S(2)}, u32[]{:S(2)}) collective-permute-start(f32[8,128]{1,0:T(8,128)S(1)} %get-tuple-element.120.vown_ref), channel_id=1, source_target_pairs={{0,1},{1,0},{2,3},{3,2},{4,5},{5,4},{6,7},{7,6},{8,9},{9,8},{10,11... | collective-permute-start | bytes 12296 | tf_op jit(solution)/shard_map/ppermute | solution.py:740
  41.5 1.2 %collective-permute-start.6 = (f32[16,128]{1,0:T(8,128)S(1)}, f32[16,128]{1,0:T(8,128)S(1)}, u32[]{:S(2)}, u32[]{:S(2)}) collective-permute-start(f32[16,128]{1,0:T(8,128)S(1)} %down_sweep.1), channel_id=1, source_target_pairs={{0,1},{1,0},{2,3},{3,2},{4,5},{5,4},{6,7},{7,6},{8,9},{9,8},{10,11... | collective-permute-start | bytes 24584 | tf_op jit(solution)/shard_map/ppermute | solution.py:745
